TPU v7x, 32 devices: a whole 2x2x4 slice. The times are simulated.
32 devices in a mesh: seq: 2 (over x), shard: 4 (over y, core), rep: 4 (over z).
Axes of the slice: x: 2, y: 2, z: 4, core: 2. Of those that a mesh axis runs over, the one named last changes fastest.
Arguments:
- tokens: bfloat16 [32, 1024, 768], P(('shard', 'rep'), 'seq'), may hold values from -6 to 6
- segment_ids: int32 [32, 1024], P(('shard', 'rep')), may hold values from 0 to 17, as said below
- out_grad: bfloat16 [32, 1024, 768], P(('shard', 'rep'), 'seq'), may hold values from -6 to 6
- norm1_gain: bfloat16 [768], P('shard'), may hold values from 0.5 to 1.5
- norm1_bias: bfloat16 [768], P('shard'), may hold values from -1.75 to 1.75
- qkv_weight: bfloat16 [768, 2304], P('shard'), may hold values from -0.21875 to 0.21875
- query_bias: bfloat16 [768], P('shard'), may hold values from -3 to 3
- value_bias: bfloat16 [768], P('shard'), may hold values from -3 to 3
- out_weight: bfloat16 [768, 768], P('shard'), may hold values from -0.625 to 0.625
- out_bias: bfloat16 [768], P('shard'), may hold values from -1.75 to 1.75
- norm2_gain: bfloat16 [768], P('shard'), may hold values from 0.5 to 1.5
- norm2_bias: bfloat16 [768], P('shard'), may hold values from -1.75 to 1.75
- ff_in_weight: bfloat16 [768, 3072], P('shard'), may hold values from -0.21875 to 0.21875
- ff_in_bias: bfloat16 [3072], P('shard'), may hold values from -3 to 3
- ff_out_weight: bfloat16 [3072, 768], P('shard'), may hold values from -0.109375 to 0.109375
- ff_out_bias: bfloat16 [768], P('shard'), may hold values from -1.75 to 1.75
Outputs:
- block_out: bfloat16 [32, 1024, 768], P(('shard', 'rep'), 'seq')
- tokens_grad: bfloat16 [32, 1024, 768], P(('shard', 'rep'), 'seq')
- norm1_gain_grad: float32 [768], P('shard')
- norm1_bias_grad: float32 [768], P('shard')
- qkv_weight_grad: float32 [768, 2304], P('shard')
- query_bias_grad: float32 [768], P('shard')
- value_bias_grad: float32 [768], P('shard')
- out_weight_grad: float32 [768, 768], P('shard')
- out_bias_grad: float32 [768], P('shard')
- norm2_gain_grad: float32 [768], P('shard')
- norm2_bias_grad: float32 [768], P('shard')
- ff_in_weight_grad: float32 [768, 3072], P('shard')
- ff_in_bias_grad: float32 [3072], P('shard')
- ff_out_weight_grad: float32 [3072, 768], P('shard')
- ff_out_bias_grad: float32 [768], P('shard')
Inputs may be any that keep to these rules, and one draw needn't show every extreme that they name: `segment_ids`: within each sequence the ids never fall; documents are numbered 1, 2, 3 and so on in order of position, each a run of 60 to 800 rows; 0 marks padding, which only follows the last document.
All inputs are finite; a program needn't handle non-finite values.
Results may differ from a plain program's by a relative error of at most 0.013.
The roundings to bfloat16 on the way count: a program that leaves them out, or rounds other values in their place, can miss the bound.
Values may be sent and summed in bfloat16 or wider, within the bound.
No kernel may reach another device: no remote copies, remote signals or barrier semaphores. Data moves between devices by JAX's collectives and lax.ppermute only.
A program may use at most 256 MiB of HBM per device.

v0:
```python
import jax
import jax.numpy as jnp
from jax import lax
from jax.sharding import PartitionSpec as P

D = 768
HEADS = 12
HEAD_DIM = 64
HEAD_GRP = 4


def norm_rows(inputs, gain_row, shift_row):
    row_mean = jnp.mean(inputs, axis=-1, keepdims=True)
    centered = inputs - row_mean
    row_var = jnp.mean(centered * centered, axis=-1, keepdims=True)
    return centered * lax.rsqrt(row_var + 1e-06) * gain_row + shift_row


def exact_gelu(inputs):
    return jax.nn.gelu(inputs, approximate=False)


def inner_rows(left, right):
    return lax.dot_general(
        left, right, (((0,), (0,)), ((), ())), preferred_element_type=jnp.float32
    )


def times_trans(left, right):
    return lax.dot_general(
        left, right, (((1,), (1,)), ((), ())), preferred_element_type=jnp.float32
    )


def head_scores(query_grp, key_grp, allowed):
    scores = jnp.einsum(
        "qhd,khd->hqk", query_grp, key_grp, preferred_element_type=jnp.float32
    ) * HEAD_DIM ** (-0.5)
    return jnp.where(allowed[None], scores, -1e30)


def forward_pass(params, token_rows, seq_ids, first_row):
    (
        n1_gain,
        n1_bias,
        w_qkv,
        q_bias,
        v_bias,
        w_out,
        o_bias,
        n2_gain,
        n2_bias,
        w_in,
        in_bias,
        w_back,
        back_bias,
    ) = params
    row_count = token_rows.shape[0]
    resid_in = token_rows.astype(jnp.float32)
    normed1 = norm_rows(resid_in, n1_gain.astype(jnp.float32), n1_bias.astype(jnp.float32)).astype(
        jnp.bfloat16
    )
    qkv_shift = jnp.concatenate([q_bias, jnp.zeros_like(q_bias), v_bias]).astype(jnp.float32)
    qkv_rows = (jnp.dot(normed1, w_qkv, preferred_element_type=jnp.float32) + qkv_shift).astype(
        jnp.bfloat16
    )
    kv_whole = lax.all_gather(qkv_rows[:, D:], "seq", axis=0, tiled=True)
    own_ids = lax.dynamic_slice_in_dim(seq_ids, first_row, row_count)
    allowed = own_ids[:, None] == seq_ids[None, :]
    group_cols = HEAD_GRP * HEAD_DIM
    mixed_parts, top_parts, total_parts = ([], [], [])
    for head_group in range(HEADS // HEAD_GRP):
        col_lo = head_group * group_cols
        query_grp = qkv_rows[:, col_lo : col_lo + group_cols].reshape(row_count, HEAD_GRP, HEAD_DIM)
        key_grp = kv_whole[:, col_lo : col_lo + group_cols].reshape(-1, HEAD_GRP, HEAD_DIM)
        value_grp = kv_whole[:, D + col_lo : D + col_lo + group_cols].reshape(
            -1, HEAD_GRP, HEAD_DIM
        )
        scores = head_scores(query_grp, key_grp, allowed)
        top_val = jnp.max(scores, axis=-1, keepdims=True)
        expo = jnp.exp(scores - top_val)
        total_val = jnp.sum(expo, axis=-1, keepdims=True)
        probs_low = (expo / total_val).astype(jnp.bfloat16)
        mixed = jnp.einsum("hqk,khd->qhd", probs_low, value_grp, preferred_element_type=jnp.float32)
        mixed_parts.append(mixed.reshape(row_count, group_cols))
        top_parts.append(top_val)
        total_parts.append(total_val)
    attn = jnp.concatenate(mixed_parts, axis=1).astype(jnp.bfloat16)
    resid_mid = (
        resid_in
        + jnp.dot(attn, w_out, preferred_element_type=jnp.float32)
        + o_bias.astype(jnp.float32)
    )
    normed2 = norm_rows(resid_mid, n2_gain.astype(jnp.float32), n2_bias.astype(jnp.float32)).astype(
        jnp.bfloat16
    )
    pre_act = jnp.dot(normed2, w_in, preferred_element_type=jnp.float32) + in_bias.astype(
        jnp.float32
    )
    hidden = exact_gelu(pre_act).astype(jnp.bfloat16)
    block_rows = (
        resid_mid
        + jnp.dot(hidden, w_back, preferred_element_type=jnp.float32)
        + back_bias.astype(jnp.float32)
    )
    kept = (
        resid_in,
        normed1,
        qkv_rows,
        kv_whole,
        top_parts,
        total_parts,
        allowed,
        attn,
        resid_mid,
        normed2,
        pre_act,
        hidden,
    )
    return (kept, block_rows.astype(jnp.bfloat16))


def backward_pass(params, kept, grad_rows):
    (
        n1_gain,
        n1_bias,
        w_qkv,
        q_bias,
        v_bias,
        w_out,
        o_bias,
        n2_gain,
        n2_bias,
        w_in,
        in_bias,
        w_back,
        back_bias,
    ) = params
    (
        resid_in,
        normed1,
        qkv_rows,
        kv_whole,
        top_parts,
        total_parts,
        allowed,
        attn,
        resid_mid,
        normed2,
        pre_act,
        hidden,
    ) = kept
    row_count = grad_rows.shape[0]
    grad_backb = jnp.sum(grad_rows, axis=0, dtype=jnp.float32)
    grad_wback = inner_rows(hidden, grad_rows)
    hidden_grad = times_trans(grad_rows, w_back)
    _, gelu_pull = jax.vjp(exact_gelu, pre_act)
    pre_grad = gelu_pull(hidden_grad)[0].astype(jnp.bfloat16)
    grad_inb = jnp.sum(pre_grad, axis=0, dtype=jnp.float32)
    grad_win = inner_rows(normed2, pre_grad)
    norm2_in_grad = times_trans(pre_grad, w_in)
    _, norm2_pull = jax.vjp(
        norm_rows, resid_mid, n2_gain.astype(jnp.float32), n2_bias.astype(jnp.float32)
    )
    mid_part, grad_n2g, grad_n2b = norm2_pull(norm2_in_grad)
    mid_grad = grad_rows.astype(jnp.float32) + mid_part
    branch_grad = mid_grad.astype(jnp.bfloat16)
    grad_ob = jnp.sum(branch_grad, axis=0, dtype=jnp.float32)
    grad_wout = inner_rows(attn, branch_grad)
    attn_grad = times_trans(branch_grad, w_out).astype(jnp.bfloat16)
    group_cols = HEAD_GRP * HEAD_DIM
    query_parts, key_parts, value_parts = ([], [], [])
    for head_group in range(HEADS // HEAD_GRP):
        col_lo = head_group * group_cols
        query_grp = qkv_rows[:, col_lo : col_lo + group_cols].reshape(row_count, HEAD_GRP, HEAD_DIM)
        key_grp = kv_whole[:, col_lo : col_lo + group_cols].reshape(-1, HEAD_GRP, HEAD_DIM)
        value_grp = kv_whole[:, D + col_lo : D + col_lo + group_cols].reshape(
            -1, HEAD_GRP, HEAD_DIM
        )
        scores = head_scores(query_grp, key_grp, allowed)
        probs = jnp.exp(scores - top_parts[head_group]) / total_parts[head_group]
        probs_low = probs.astype(jnp.bfloat16)
        attn_grp = attn_grad[:, col_lo : col_lo + group_cols].reshape(row_count, HEAD_GRP, HEAD_DIM)
        value_grad = jnp.einsum(
            "hqk,qhd->khd", probs_low, attn_grp, preferred_element_type=jnp.float32
        )
        prob_grad = jnp.einsum(
            "qhd,khd->hqk", attn_grp, value_grp, preferred_element_type=jnp.float32
        )
        row_inner = jnp.sum(prob_grad * probs, axis=-1, keepdims=True)
        score_grad = (probs * (prob_grad - row_inner)).astype(jnp.bfloat16)
        query_grad = jnp.einsum(
            "hqk,khd->qhd", score_grad, key_grp, preferred_element_type=jnp.float32
        ) * HEAD_DIM ** (-0.5)
        key_grad = jnp.einsum(
            "hqk,qhd->khd", score_grad, query_grp, preferred_element_type=jnp.float32
        ) * HEAD_DIM ** (-0.5)
        query_parts.append(query_grad.reshape(row_count, group_cols))
        key_parts.append(key_grad.reshape(-1, group_cols))
        value_parts.append(value_grad.reshape(-1, group_cols))
    kv_terms = jnp.concatenate(key_parts + value_parts, axis=1)
    kv_owned = lax.psum_scatter(kv_terms, "seq", scatter_dimension=0, tiled=True)
    qkv_grad = jnp.concatenate(
        [jnp.concatenate(query_parts, axis=1).astype(jnp.bfloat16), kv_owned.astype(jnp.bfloat16)],
        axis=1,
    )
    grad_qb = jnp.sum(qkv_grad[:, :D], axis=0, dtype=jnp.float32)
    grad_vb = jnp.sum(qkv_grad[:, 2 * D :], axis=0, dtype=jnp.float32)
    grad_qkv = inner_rows(normed1, qkv_grad)
    norm1_in_grad = times_trans(qkv_grad, w_qkv)
    _, norm1_pull = jax.vjp(
        norm_rows, resid_in, n1_gain.astype(jnp.float32), n1_bias.astype(jnp.float32)
    )
    in_part, grad_n1g, grad_n1b = norm1_pull(norm1_in_grad)
    token_grad = (mid_grad + in_part).astype(jnp.bfloat16)
    terms = (
        grad_n1g,
        grad_n1b,
        grad_qkv,
        grad_qb,
        grad_vb,
        grad_wout,
        grad_ob,
        grad_n2g,
        grad_n2b,
        grad_win,
        grad_inb,
        grad_wback,
        grad_backb,
    )
    return (terms, token_grad)


def body(
    tokens,
    segment_ids,
    out_grad,
    norm1_gain,
    norm1_bias,
    qkv_weight,
    query_bias,
    value_bias,
    out_weight,
    out_bias,
    norm2_gain,
    norm2_bias,
    ff_in_weight,
    ff_in_bias,
    ff_out_weight,
    ff_out_bias,
):
    shards = (
        norm1_gain,
        norm1_bias,
        qkv_weight,
        query_bias,
        value_bias,
        out_weight,
        out_bias,
        norm2_gain,
        norm2_bias,
        ff_in_weight,
        ff_in_bias,
        ff_out_weight,
        ff_out_bias,
    )
    first_row = lax.axis_index("seq") * tokens.shape[1]
    micro_count = tokens.shape[0]
    out_list, grad_list = ([], [])
    totals = None
    for micro_idx in range(micro_count):
        params = (
            lax.all_gather(shards[0], "shard", axis=0, tiled=True),
            lax.all_gather(shards[1], "shard", axis=0, tiled=True),
            lax.all_gather(shards[2], "shard", axis=0, tiled=True),
            lax.all_gather(shards[3], "shard", axis=0, tiled=True),
            lax.all_gather(shards[4], "shard", axis=0, tiled=True),
            lax.all_gather(shards[5], "shard", axis=0, tiled=True),
            lax.all_gather(shards[6], "shard", axis=0, tiled=True),
            lax.all_gather(shards[7], "shard", axis=0, tiled=True),
            lax.all_gather(shards[8], "shard", axis=0, tiled=True),
            lax.all_gather(shards[9], "shard", axis=0, tiled=True),
            lax.all_gather(shards[10], "shard", axis=0, tiled=True),
            lax.all_gather(shards[11], "shard", axis=0, tiled=True),
            lax.all_gather(shards[12], "shard", axis=0, tiled=True),
        )
        kept, block_rows = forward_pass(
            params, tokens[micro_idx], segment_ids[micro_idx], first_row
        )
        params = (
            lax.all_gather(shards[0], "shard", axis=0, tiled=True),
            lax.all_gather(shards[1], "shard", axis=0, tiled=True),
            lax.all_gather(shards[2], "shard", axis=0, tiled=True),
            lax.all_gather(shards[3], "shard", axis=0, tiled=True),
            lax.all_gather(shards[4], "shard", axis=0, tiled=True),
            lax.all_gather(shards[5], "shard", axis=0, tiled=True),
            lax.all_gather(shards[6], "shard", axis=0, tiled=True),
            lax.all_gather(shards[7], "shard", axis=0, tiled=True),
            lax.all_gather(shards[8], "shard", axis=0, tiled=True),
            lax.all_gather(shards[9], "shard", axis=0, tiled=True),
            lax.all_gather(shards[10], "shard", axis=0, tiled=True),
            lax.all_gather(shards[11], "shard", axis=0, tiled=True),
            lax.all_gather(shards[12], "shard", axis=0, tiled=True),
        )
        terms, token_grad = backward_pass(params, kept, out_grad[micro_idx])
        if micro_idx == 0:
            totals = terms
        else:
            totals = jax.tree.map(jnp.add, totals, terms)
        out_list.append(block_rows)
        grad_list.append(token_grad)
    out_stack = jnp.stack(out_list)
    grad_stack = jnp.stack(grad_list)
    owned = lax.psum_scatter(totals, "shard", scatter_dimension=0, tiled=True)
    summed = lax.psum(owned, ("seq", "rep"))
    return (out_stack, grad_stack) + tuple(summed)


def solution(mesh):
    in_specs = (
        P(("shard", "rep"), "seq", None),
        P(("shard", "rep"), None),
        P(("shard", "rep"), "seq", None),
        P("shard"),
        P("shard"),
        P("shard", None),
        P("shard"),
        P("shard"),
        P("shard", None),
        P("shard"),
        P("shard"),
        P("shard"),
        P("shard", None),
        P("shard"),
        P("shard", None),
        P("shard"),
    )
    out_specs = (
        P(("shard", "rep"), "seq", None),
        P(("shard", "rep"), "seq", None),
        P("shard"),
        P("shard"),
        P("shard", None),
        P("shard"),
        P("shard"),
        P("shard", None),
        P("shard"),
        P("shard"),
        P("shard"),
        P("shard", None),
        P("shard"),
        P("shard", None),
        P("shard"),
    )
    return jax.shard_map(body, mesh=mesh, in_specs=in_specs, out_specs=out_specs, check_vma=False)
```

profile of v0, /device:TPU:0, one launch (start us, length us, event | category | flops | bytes accessed | tf_op | source)
XLA Modules:
  0.0 1060.4 jit_solution(15221362379857821363)
XLA Ops:
  16.7 14.0 %all-reduce.20 = (bf16[768]{0:T(1024)(128)(2,1)S(1)}, bf16[768]{0:T(1024)(128)(2,1)S(1)}, bf16[768]{0:T(1024)(128)(2,1)S(1)}, bf16[768]{0:T(1024)(128)(2,1)S(1)}...) all-reduce(bf16[768]{0:T(1024)(128)(2,1)S(1)} %dynamic-update-slice, ...), channel_id=1, replica_groups=mesh['seq'=2,'shard'=4,'rep'=4] {'shard'}, use_global_device_ids=true, to_apply=%add.4 | all-reduce | flops 6144 | bytes 24576
  34.9 8.4 all-gather.8.cloned.1.call-done
  59.1 5.4 all-gather
  73.6 21.7 %all-gather.18.cloned.1.call-done = bf16[1024,1536]{1,0:T(8,128)(2,1)} async-done(((bf16[512,1536]{1,0:T(8,128)(2,1)}), bf16[1024,1536]{1,0:T(8,128)(2,1)}) %all-gather.18.cloned.1.call-update) | async-done | bytes 3145744 | tf_op jit(solution)/shard_map/all_gather | solution.py:67
  106.9 35.5 %all-gather.10.cloned.1.call-done = bf16[1024,1536]{1,0:T(8,128)(2,1)} async-done(((bf16[512,1536]{1,0:T(8,128)(2,1)}), bf16[1024,1536]{1,0:T(8,128)(2,1)}) %all-gather.10.cloned.1.call-update) | async-done | bytes 3145744 | tf_op jit(solution)/shard_map/all_gather | solution.py:67
  158.3 7.5 fusion.208
  165.9 7.9 fusion.207
  173.7 20.3 %fusion.209 = (f32[4,512]{1,0:T(4,128)S(1)}, f32[4,512,1024]{2,1,0:T(8,128)}) fusion(pred[512,1024]{1,0:T(8,128)(4,1)} %broadcast_compare_fusion.1, bf16[512,4,64]{0,2,1:T(8,128)(2,1)} %bitcast.358, bf16[1024,4,64]{0,2,1:T(8,128)(2,1)} %bitcast.348), kind=kOutput, calls=%fused_computation.322 | convolution fusion | flops 276825088 | bytes 9707520 | tf_op jit(solution)/shard_map/sub | solution.py:81
  194.1 5.9 fusion.101
  209.8 6.4 fusion.205
  216.2 7.5 fusion.204
  223.7 5.3 fusion.206
  229.1 5.0 fusion.110
  240.7 4.9 fusion.189
  248.3 35.2 %multiply_convert_fusion.7 = (bf16[512,3072]{1,0:T(8,128)(2,1)}, f32[512,3072]{1,0:T(8,128)}, bf16[512,3072]{1,0:T(8,128)(2,1)}, f32[512,3072]{1,0:T(8,128)}, f32[512,3072]{1,0:T(8,128)}) fusion(f32[3072]{0:T(1024)S(1)} %bitcast.413, f32[512,3072]{1,0:T(8,128)S(1)} %fusion.189, bf16[768,3072]{1,0:T(8,128)(2,1)S(1)} %copy-done.151, ...), kind=kOutput, calls=%fused_computation.57 | convolution fusion | flops 2625503232 | bytes 37771264 | tf_op jit(solution)/shard_map/dot_general | solution.py:97
  283.5 9.2 convert_reduce_fusion
  296.2 9.2 convert_reduce_fusion.1
  305.4 5.7 multiply_reduce_fusion.7
  316.1 4.4 fusion.44
  320.4 6.3 multiply_reduce_fusion
  327.0 4.4 fusion.48
  331.3 6.3 multiply_reduce_fusion.1
  337.8 4.4 fusion.52
  342.2 6.4 multiply_reduce_fusion.2
  354.7 6.6 multiply_convert_fusion
  364.6 4.4 multiply_convert_fusion.1
  369.9 4.9 multiply_convert_fusion.2
  383.0 4.9 multiply_reduce_fusion.5
  392.7 8.2 multiply_reduce_fusion.4
  402.5 4.3 multiply_convert_fusion.4
  409.2 4.2 multiply_reduce_fusion.3
  413.4 4.2 multiply_convert_fusion.3
  431.3 5.0 fusion.187
  436.3 5.9 convolution_add_fusion.2
  443.7 4.8 fusion.143
  448.5 5.3 convolution_add_fusion.1
  454.8 4.4 fusion.118
  472.8 67.0 %reduce-scatter.7.cloned.1.call-done = f32[512,1536]{0,1:T(8,128)} async-done(((f32[1024,1536]{0,1:T(8,128)}), f32[512,1536]{0,1:T(8,128)}) %reduce-scatter.7.cloned.1.call-update) | async-done | bytes 3145744 | tf_op jit(solution)/shard_map/reduce_scatter | solution.py:202
  544.6 5.3 convolution_add_fusion
  550.2 25.8 %reduce-scatter.13.cloned.1.call-done = f32[192,768]{1,0:T(8,128)} async-done(((f32[768,768]{1,0:T(8,128)}), f32[192,768]{1,0:T(8,128)}) %reduce-scatter.13.cloned.1.call-update) | async-done | bytes 589840 | tf_op jit(solution)/shard_map/reduce_scatter | solution.py:314
  576.0 81.1 %reduce-scatter.15.cloned.1.call-done = f32[192,3072]{1,0:T(8,128)} async-done(((f32[768,3072]{1,0:T(8,128)}), f32[192,3072]{1,0:T(8,128)}) %reduce-scatter.15.cloned.1.call-update) | async-done | bytes 2359312 | tf_op jit(solution)/shard_map/reduce_scatter | solution.py:314
  657.2 81.2 %reduce-scatter.17.cloned.1.call-done = f32[768,768]{1,0:T(8,128)} async-done(((f32[3072,768]{1,0:T(8,128)}), f32[768,768]{1,0:T(8,128)}) %reduce-scatter.17.cloned.1.call-update) | async-done | bytes 2359312 | tf_op jit(solution)/shard_map/reduce_scatter | solution.py:314
  738.3 66.3 %reduce-scatter.11.cloned.1.call-done = f32[192,2304]{1,0:T(8,128)} async-done(((f32[768,2304]{1,0:T(8,128)}), f32[192,2304]{1,0:T(8,128)}) %reduce-scatter.11.cloned.1.call-update) | async-done | bytes 1769488 | tf_op jit(solution)/shard_map/reduce_scatter | solution.py:314
  808.6 6.5 fusion.96
  815.1 5.1 fusion.97
  828.6 12.0 %all-reduce.19 = (f32[768]{0:T(1024)S(1)}, f32[768]{0:T(1024)S(1)}, f32[768]{0:T(1024)S(1)}, f32[768]{0:T(1024)S(1)}, f32[768]{0:T(1024)S(1)}, /*index=5*/f32[76...) all-reduce(f32[768]{0:T(1024)S(1)} %add.282, ...), channel_id=4, replica_groups=mesh['seq'=2,'shard'=4,'rep'=4] {'shard'}, use_global_device_ids=true, to_apply=%region_38.39.clone | all-reduce | flops 9216 | bytes 73728
  841.3 39.8 %all-reduce.17 = (f32[192]{0:T(256)}, f32[192]{0:T(256)}, f32[192]{0:T(256)}, f32[192]{0:T(256)}, f32[192]{0:T(256)}, /*index=5*/f32[192]{0:T(256)}, f32[192]{0:T(256)}, f32[768]{0:T(1024)}, f32[192]{0:T(256)}) all-reduce(f32[192]{0:T(256)S(1)} %dynamic-slice.11, ...), channel_id=1, replica_groups=mesh['seq'=2,'shard'=4,'rep'=4] {'seq','rep'}, use_global_device_ids=true, to_apply=%region_39.40 | all-reduce | flops 2304 | bytes 18432 | tf_op jit(solution)/shard_map/psum | solution.py:315
  886.0 160.0 %all-reduce.23.cloned.1.call-done = (f32[192,2304]{1,0:T(8,128)}, f32[192,768]{1,0:T(8,128)}, f32[192,3072]{1,0:T(8,128)}, f32[768,768]{1,0:T(8,128)}) async-done(((f32[192,2304]{1,0:T(8,128)}, f32[192,768]{1,0:T(8,128)}, f32[192,3072]{1,0:T(8,128)}, f32[768,768]{1,0:T(8,128)}), (f32[192,2304]{1,0:T(8,128)}, f32[192,768]{1,0:T(8,128)}, f32[192,3072]{1,0:T(8,128)}, ...) | async-done | bytes 7077904 | tf_op jit(solution)/shard_map/psum | solution.py:315
  (546 shorter events, 177.5 us)
Async XLA Ops:
  7.2 36.1 %copy-start.11 = (bf16[2,512,768]{2,1,0:T(8,128)(2,1)S(1)}, bf16[2,512,768]{2,1,0:T(8,128)(2,1)}, u32[]{:S(2)}) copy-start(bf16[2,512,768]{2,1,0:T(8,128)(2,1)} %param.16) | copy-start | bytes 4718596
  7.2 36.1 %all-gather.8.cloned.1.call-start = ((), (), s32[]{:S(2)}) async-start(), calls=%async_computation.6 | async-start | bytes 4423680 | tf_op jit(solution)/shard_map/all_gather | solution.py:275
  7.9 87.4 %all-gather.18.cloned.1.call-start = ((), (), s32[]{:S(2)}) async-start(), calls=%async_computation.11 | async-start | bytes 4718592 | tf_op jit(solution)/shard_map/all_gather | solution.py:67
  30.7 19.6 %copy-start.97 = (f32[768]{0:T(1024)}, f32[768]{0:T(1024)S(1)}, u32[]{:S(2)}) copy-start(f32[768]{0:T(1024)S(1)} %convert_element_type.193) | copy-start | bytes 9220
  50.2 92.2 %all-gather.10.cloned.1.call-start = ((), (), s32[]{:S(2)}) async-start(), calls=%async_computation.7 | async-start | bytes 4718592 | tf_op jit(solution)/shard_map/all_gather | solution.py:67
  57.2 148.1 %all-gather.12.cloned.1.call-start = ((), (), s32[]{:S(2)}) async-start(), calls=%async_computation.8 | async-start | bytes 1474560 | tf_op jit(solution)/shard_map/all_gather | solution.py:278
  57.7 182.9 %all-gather.14.cloned.1.call-start = ((), (), s32[]{:S(2)}) async-start(), calls=%async_computation.9 | async-start | bytes 5898240 | tf_op jit(solution)/shard_map/all_gather | solution.py:282
  58.3 225.2 %all-gather.16.cloned.1.call-start = ((), (), s32[]{:S(2)}) async-start(), calls=%async_computation.10 | async-start | bytes 5898240 | tf_op jit(solution)/shard_map/all_gather | solution.py:284
  58.9 410.3 %reduce-scatter.9.cloned.1.call-start = ((), (), s32[]{:S(2)}) async-start(), calls=%async_computation.13 | async-start | bytes 9437184 | tf_op jit(solution)/shard_map/reduce_scatter | solution.py:202
  59.0 252.2 %copy-start.101 = (f32[768]{0:T(1024)}, f32[768]{0:T(1024)S(1)}, u32[]{:S(2)}) copy-start(f32[768]{0:T(1024)S(1)} %convert_element_type.201) | copy-start | bytes 9220
  59.0 186.6 %copy-start.103 = (f32[768]{0:T(1024)}, f32[768]{0:T(1024)S(1)}, u32[]{:S(2)}) copy-start(f32[768]{0:T(1024)S(1)} %convert_element_type.202) | copy-start | bytes 9220
  72.7 93.1 %copy-start.55 = (bf16[512,256]{0,1:T(8,128)(2,1)}, bf16[512,256]{0,1:T(8,128)(2,1)S(1)}, u32[]{:S(2)}) copy-start(bf16[512,256]{0,1:T(8,128)(2,1)S(1)} %copy.110) | copy-start | bytes 786436
  98.8 124.9 %copy-start.46 = (bf16[1024,256]{0,1:T(8,128)(2,1)}, bf16[1024,256]{0,1:T(8,128)(2,1)S(1)}, u32[]{:S(2)}) copy-start(bf16[1024,256]{0,1:T(8,128)(2,1)S(1)} %copy.114) | copy-start | bytes 1572868
  100.2 115.9 %copy-start.48 = (bf16[1024,256]{0,1:T(8,128)(2,1)}, bf16[1024,256]{0,1:T(8,128)(2,1)S(1)}, u32[]{:S(2)}) copy-start(bf16[1024,256]{0,1:T(8,128)(2,1)S(1)} %copy.120) | copy-start | bytes 1572868
  102.5 107.3 %copy-start.50 = (bf16[1024,256]{0,1:T(8,128)(2,1)}, bf16[1024,256]{0,1:T(8,128)(2,1)S(1)}, u32[]{:S(2)}) copy-start(bf16[1024,256]{0,1:T(8,128)(2,1)S(1)} %copy.117) | copy-start | bytes 1572868
  165.8 28.2 %copy-start.133 = (f32[4,512]{1,0:T(4,128)}, f32[4,512]{1,0:T(4,128)S(1)}, u32[]{:S(2)}) copy-start(f32[4,512]{1,0:T(4,128)S(1)} %get-tuple-element.128) | copy-start | bytes 24580
  173.7 26.3 %copy-start.131 = (f32[4,512]{1,0:T(4,128)}, f32[4,512]{1,0:T(4,128)S(1)}, u32[]{:S(2)}) copy-start(f32[4,512]{1,0:T(4,128)S(1)} %get-tuple-element.126) | copy-start | bytes 24580
  207.8 103.4 %copy-start.117 = (f32[512]{0:T(512)}, f32[512]{0:T(512)S(1)}, u32[]{:S(2)}) copy-start(f32[512]{0:T(512)S(1)} %broadcast_multiply_fusion.2) | copy-start | bytes 6148
  209.8 101.4 %copy-start.141 = (f32[512]{0:T(512)}, f32[512]{0:T(512)S(1)}, u32[]{:S(2)}) copy-start(f32[512]{0:T(512)S(1)} %fusion.158) | copy-start | bytes 6148
  240.3 70.9 %copy-start.13 = (f32[512,768]{1,0:T(8,128)}, f32[512,768]{1,0:T(8,128)S(1)}, u32[]{:S(2)}) copy-start(f32[512,768]{1,0:T(8,128)S(1)} %get-tuple-element.135) | copy-start | bytes 4718596
  240.3 70.9 %copy-start.105 = (f32[512]{0:T(512)}, f32[512]{0:T(512)S(1)}, u32[]{:S(2)}) copy-start(f32[512]{0:T(512)S(1)} %broadcast_multiply_fusion) | copy-start | bytes 6148
  240.6 70.6 %copy-start.109 = (f32[512]{0:T(512)}, f32[512]{0:T(512)S(1)}, u32[]{:S(2)}) copy-start(f32[512]{0:T(512)S(1)} %fusion.160) | copy-start | bytes 6148
  248.3 35.2 %copy-start.18 = (bf16[2,512,768]{2,1,0:T(8,128)(2,1)S(1)}, bf16[2,512,768]{2,1,0:T(8,128)(2,1)}, u32[]{:S(2)}) copy-start(bf16[2,512,768]{2,1,0:T(8,128)(2,1)} %param.18) | copy-start | bytes 4718596
  382.6 157.3 %reduce-scatter.7.cloned.1.call-start = ((), (), s32[]{:S(2)}) async-start(), calls=%async_computation.12 | async-start | bytes 9437184 | tf_op jit(solution)/shard_map/reduce_scatter | solution.py:202
  426.9 149.1 %reduce-scatter.13.cloned.1.call-start = ((), (), s32[]{:S(2)}) async-start(), calls=%async_computation.15 | async-start | bytes 2949120 | tf_op jit(solution)/shard_map/reduce_scatter | solution.py:314
  430.8 226.3 %reduce-scatter.15.cloned.1.call-start = ((), (), s32[]{:S(2)}) async-start(), calls=%async_computation.16 | async-start | bytes 11796480 | tf_op jit(solution)/shard_map/reduce_scatter | solution.py:314
  442.3 296.0 %reduce-scatter.17.cloned.1.call-start = ((), (), s32[]{:S(2)}) async-start(), calls=%async_computation.17 | async-start | bytes 11796480 | tf_op jit(solution)/shard_map/reduce_scatter | solution.py:314
  453.8 350.8 %reduce-scatter.11.cloned.1.call-start = ((), (), s32[]{:S(2)}) async-start(), calls=%async_computation.14 | async-start | bytes 8847360 | tf_op jit(solution)/shard_map/reduce_scatter | solution.py:314
  469.2 72.8 %copy-start.12 = (bf16[2,512,768]{2,1,0:T(8,128)(2,1)S(1)}, bf16[2,512,768]{2,1,0:T(8,128)(2,1)}, u32[]{:S(2)}) copy-start(bf16[2,512,768]{2,1,0:T(8,128)(2,1)} %param.16) | copy-start | bytes 4718596
  469.2 72.9 %copy-start.85 = (f32[768]{0:T(1024)S(1)}, f32[768]{0:T(1024)}, u32[]{:S(2)}) copy-start(f32[768]{0:T(1024)} %copy-done.84) | copy-start | bytes 9220
  469.2 72.9 %copy-start.98 = (f32[768]{0:T(1024)S(1)}, f32[768]{0:T(1024)}, u32[]{:S(2)}) copy-start(f32[768]{0:T(1024)} %copy-done.97) | copy-start | bytes 9220
  469.2 72.9 %copy-start.108 = (f32[512]{0:T(512)S(1)}, f32[512]{0:T(512)}, u32[]{:S(2)}) copy-start(f32[512]{0:T(512)} %copy-done.107) | copy-start | bytes 6148
  469.2 72.9 %copy-start.112 = (f32[512]{0:T(512)S(1)}, f32[512]{0:T(512)}, u32[]{:S(2)}) copy-start(f32[512]{0:T(512)} %copy-done.111) | copy-start | bytes 6148
  549.9 256.0 %copy-start.148 = (bf16[768]{0:T(1024)(128)(2,1)S(1)}, bf16[768]{0:T(1024)(128)(2,1)}, u32[]{:S(2)}) copy-start(bf16[768]{0:T(1024)(128)(2,1)} %get-tuple-element.66) | copy-start | bytes 4612
  549.9 256.0 %copy-start.129 = (f32[3072]{0:T(1024)S(1)}, f32[3072]{0:T(1024)}, u32[]{:S(2)}) copy-start(f32[3072]{0:T(1024)} %get-tuple-element.153) | copy-start | bytes 36868
  549.9 256.0 %copy-start.130 = (f32[3072]{0:T(1024)S(1)}, f32[3072]{0:T(1024)}, u32[]{:S(2)}) copy-start(f32[3072]{0:T(1024)} %get-tuple-element.151) | copy-start | bytes 36868
  549.9 256.0 %copy-start.146 = (f32[768]{0:T(1024)S(1)}, f32[768]{0:T(1024)}, u32[]{:S(2)}) copy-start(f32[768]{0:T(1024)} %get-tuple-element.21) | copy-start | bytes 9220
  549.9 256.0 %copy-start.147 = (f32[768]{0:T(1024)S(1)}, f32[768]{0:T(1024)}, u32[]{:S(2)}) copy-start(f32[768]{0:T(1024)} %get-tuple-element.117) | copy-start | bytes 9220
  549.9 256.0 %copy-start.144 = (f32[768]{0:T(1024)S(1)}, f32[768]{0:T(1024)}, u32[]{:S(2)}) copy-start(f32[768]{0:T(1024)} %get-tuple-element.31) | copy-start | bytes 9220
  549.9 256.0 %copy-start.145 = (f32[768]{0:T(1024)S(1)}, f32[768]{0:T(1024)}, u32[]{:S(2)}) copy-start(f32[768]{0:T(1024)} %get-tuple-element.115) | copy-start | bytes 9220
  549.9 256.1 %copy-start.127 = (f32[768]{0:T(1024)S(1)}, f32[768]{0:T(1024)}, u32[]{:S(2)}) copy-start(f32[768]{0:T(1024)} %get-tuple-element.28) | copy-start | bytes 9220
  550.0 256.1 %copy-start.128 = (f32[768]{0:T(1024)S(1)}, f32[768]{0:T(1024)}, u32[]{:S(2)}) copy-start(f32[768]{0:T(1024)} %get-tuple-element.29) | copy-start | bytes 9220
  550.0 256.1 %copy-start.125 = (f32[768]{0:T(1024)S(1)}, f32[768]{0:T(1024)}, u32[]{:S(2)}) copy-start(f32[768]{0:T(1024)} %get-tuple-element.99) | copy-start | bytes 9220
  550.0 256.1 %copy-start.126 = (f32[768]{0:T(1024)S(1)}, f32[768]{0:T(1024)}, u32[]{:S(2)}) copy-start(f32[768]{0:T(1024)} %get-tuple-element.101) | copy-start | bytes 9220
  550.0 495.9 %all-reduce.23.cloned.1.call-start = ((), (), s32[]{:S(2)}) async-start(), calls=%async_computation.18 | async-start | bytes 14155776 | tf_op jit(solution)/shard_map/psum | solution.py:315
  826.4 54.6 %copy-start.16 = (f32[512,768]{1,0:T(8,128)S(1)}, f32[512,768]{1,0:T(8,128)}, u32[]{:S(2)}) copy-start(f32[512,768]{1,0:T(8,128)} %copy-done.15) | copy-start | bytes 4718596
  826.4 54.6 %copy-start.114 = (f32[512]{0:T(512)S(1)}, f32[512]{0:T(512)}, u32[]{:S(2)}) copy-start(f32[512]{0:T(512)} %copy-done.113) | copy-start | bytes 6148
  826.5 54.6 %copy-start.116 = (f32[512]{0:T(512)S(1)}, f32[512]{0:T(512)}, u32[]{:S(2)}) copy-start(f32[512]{0:T(512)} %copy-done.115) | copy-start | bytes 6148
  (140 other events, 663.7 us)
Sparse Core Ops, SparseCore 0:
  9.6 33.6 all-gather.7
  50.3 44.9 all-gather.17
  97.4 44.9 all-gather.9
  143.8 17.4 all-gather.11
  162.7 37.4 all-gather.13
  201.6 37.4 all-gather.15
  382.7 77.5 reduce-scatter.8
  462.7 77.0 reduce-scatter.6
  543.0 33.0 reduce-scatter.12
  578.7 78.4 reduce-scatter.14
  659.9 78.3 reduce-scatter.16
  740.9 63.6 reduce-scatter.10
  809.0 236.8 all-reduce.22
where the time goes:
time: 1060 us
  waiting for transfers between devices  549 us (52%)
  matrix products  274 us (26%)
  local copies, waits for them, and re-layouts  93.7 us (9%)
  blocking collectives  71.2 us (7%)
  other arithmetic  52.6 us (5%)
  between operations  18.5 us (2%)
    reduce_scatter x4, waiting for transfers between devices, body(): owned = lax.psum_scatter(totals, 'shard', scatter_dimension=0, tiled=True)  254 us
    psum x1, waiting for transfers between devices, body(): summed = lax.psum(owned, ('seq', 'rep'))  160 us
    reduce_scatter x2, waiting for transfers between devices, backward_pass(): lax.psum_scatter(kv_terms, 'seq', scatter_dimension=0, tiled=True)  67.1 us
    all_gather x2, waiting for transfers between devices, forward_pass(): kv_whole = lax.all_gather(qkv_rows[:, D:], 'seq', axis=0, tiled=True)  57.2 us
    sub x6, matrix products, forward_pass(): expo = jnp.exp(scores - top_val)  54.9 us
    unnamed x392, local copies, waits for them, and re-layouts  49.1 us
    dot_general x2, matrix products, forward_pass(): jnp.dot(normed2, w_in, preferred_element_type=jnp.float32)  40.1 us
    psum x1, blocking collectives, body(): summed = lax.psum(owned, ('seq', 'rep'))  39.8 us
  transfers between devices with their start and end apart: 13, of which 9 were waited for; matrix products, arithmetic and copies ran while one was open for 27% of the time, Pallas kernels for 0%

commit v1 on v0

v1 whole, which is shorter than its diff:
```python
import jax
import jax.numpy as jnp
from jax import lax
from jax.sharding import PartitionSpec as P

D = 768
HEADS = 12
HEAD_DIM = 64
HEAD_GRP = 4
BF = jnp.bfloat16
F32 = jnp.float32


def xor_send(value, axis, mask):
    size = lax.axis_size(axis)
    return lax.ppermute(value, axis, [(i, i ^ mask) for i in range(size)])


def pick(stacked, index):
    return lax.dynamic_index_in_dim(stacked, index, 0, keepdims=False)


def reduce_shard(grad):
    size = lax.axis_size("shard")
    me = lax.axis_index("shard")
    rows = grad.shape[0] // size
    part = grad.reshape(size, rows, grad.shape[1])
    bit = 1
    while bit < size:
        split = part.reshape(part.shape[0] // 2, 2, rows, grad.shape[1])
        own = (me // bit) % 2
        sent = lax.dynamic_index_in_dim(split, 1 - own, 1, keepdims=False).astype(BF)
        kept = lax.dynamic_index_in_dim(split, own, 1, keepdims=False)
        part = kept + xor_send(sent, "shard", bit).astype(F32)
        bit *= 2
    return part[0]


def scatter_axis(part, axis):
    size = lax.axis_size(axis)
    me = lax.axis_index(axis)
    pieces = part.reshape(size, part.shape[0] // size, part.shape[1])
    total = pick(pieces, me)
    for mask in range(1, size):
        total = total + xor_send(pick(pieces, me ^ mask).astype(BF), axis, mask).astype(F32)
    return total


def gather_axis(piece, axis):
    size = lax.axis_size(axis)
    me = lax.axis_index(axis)
    rows = piece.shape[0]
    whole = jnp.zeros((size * rows, piece.shape[1]), piece.dtype)
    whole = lax.dynamic_update_slice(whole, piece, (me * rows, 0))
    for mask in range(1, size):
        whole = lax.dynamic_update_slice(
            whole, xor_send(piece, axis, mask), ((me ^ mask) * rows, 0)
        )
    return whole


def reduce_grad(grad):
    part = reduce_shard(grad)
    part = scatter_axis(part, "seq")
    part = scatter_axis(part, "rep").astype(BF)
    part = gather_axis(part, "rep")
    return gather_axis(part, "seq").astype(F32)


def sum_all(value):
    for axis in ("shard", "seq", "rep"):
        bit = 1
        while bit < lax.axis_size(axis):
            value = value + xor_send(value, axis, bit)
            bit *= 2
    return value


def norm_stats(inputs):
    row_mean = jnp.mean(inputs, axis=-1, keepdims=True)
    centered = inputs - row_mean
    row_var = jnp.mean(centered * centered, axis=-1, keepdims=True)
    rstd = lax.rsqrt(row_var + 1e-06)
    return centered * rstd, rstd


def norm_back(in_grad, normal, rstd, gain):
    scaled = in_grad * gain
    mean_e = jnp.mean(scaled, axis=-1, keepdims=True)
    mean_en = jnp.mean(scaled * normal, axis=-1, keepdims=True)
    return rstd * (scaled - mean_e - normal * mean_en)


def inner_rows(left, right):
    return lax.dot_general(
        left, right, (((0,), (0,)), ((), ())), preferred_element_type=jnp.float32
    )


def times_trans(left, right):
    return lax.dot_general(
        left, right, (((1,), (1,)), ((), ())), preferred_element_type=jnp.float32
    )


def times(left, right):
    return jnp.dot(left, right, preferred_element_type=jnp.float32)


def head_scores(query_grp, key_grp, allowed):
    scores = jnp.einsum(
        "qhd,khd->hqk", query_grp, key_grp, preferred_element_type=jnp.float32
    ) * HEAD_DIM ** (-0.5)
    return jnp.where(allowed[None], scores, -1e30)


def attention(qkv_rows, ids):
    rows = qkv_rows.shape[0]
    allowed = ids[:, None] == ids[None, :]
    cols = HEAD_GRP * HEAD_DIM
    mixed_parts, lse_parts = [], []
    for group in range(HEADS // HEAD_GRP):
        lo = group * cols
        query_grp, key_grp, value_grp = (
            qkv_rows[:, at + lo : at + lo + cols].reshape(rows, HEAD_GRP, HEAD_DIM)
            for at in (0, D, 2 * D)
        )
        scores = head_scores(query_grp, key_grp, allowed)
        top = jnp.max(scores, axis=-1, keepdims=True)
        expo = jnp.exp(scores - top)
        total = jnp.sum(expo, axis=-1, keepdims=True)
        probs_low = (expo / total).astype(BF)
        mixed = jnp.einsum("hqk,khd->qhd", probs_low, value_grp, preferred_element_type=F32)
        mixed_parts.append(mixed.reshape(rows, cols))
        lse_parts.append(top + jnp.log(total))
    return jnp.concatenate(mixed_parts, axis=1).astype(BF), lse_parts


def attention_back(qkv_rows, ids, attn, lse_parts, attn_grad):
    rows = qkv_rows.shape[0]
    allowed = ids[:, None] == ids[None, :]
    cols = HEAD_GRP * HEAD_DIM
    query_parts, key_parts, value_parts = [], [], []
    for group in range(HEADS // HEAD_GRP):
        lo = group * cols
        query_grp, key_grp, value_grp = (
            qkv_rows[:, at + lo : at + lo + cols].reshape(rows, HEAD_GRP, HEAD_DIM)
            for at in (0, D, 2 * D)
        )
        probs = jnp.exp(head_scores(query_grp, key_grp, allowed) - lse_parts[group])
        probs_low = probs.astype(BF)
        attn_grp = attn_grad[:, lo : lo + cols].reshape(rows, HEAD_GRP, HEAD_DIM)
        value_grad = jnp.einsum("hqk,qhd->khd", probs_low, attn_grp, preferred_element_type=F32)
        prob_grad = jnp.einsum("qhd,khd->hqk", attn_grp, value_grp, preferred_element_type=F32)
        row_inner = jnp.sum(prob_grad * probs, axis=-1, keepdims=True)
        score_grad = (probs * (prob_grad - row_inner)).astype(BF)
        query_grad = jnp.einsum("hqk,khd->qhd", score_grad, key_grp, preferred_element_type=F32)
        key_grad = jnp.einsum("hqk,qhd->khd", score_grad, query_grp, preferred_element_type=F32)
        scale = HEAD_DIM ** (-0.5)
        query_parts.append((query_grad * scale).reshape(rows, cols))
        key_parts.append((key_grad * scale).reshape(rows, cols))
        value_parts.append(value_grad.reshape(rows, cols))
    return jnp.concatenate(query_parts + key_parts + value_parts, axis=1).astype(BF)


def swap_halves(halves, me):
    size = lax.axis_size("seq")
    whole = jnp.zeros_like(halves)
    whole = lax.dynamic_update_slice(whole, pick(halves, me)[None], (me, 0, 0))
    for mask in range(1, size):
        got = xor_send(pick(halves, me ^ mask), "seq", mask)
        whole = lax.dynamic_update_slice(whole, got[None], (me ^ mask, 0, 0))
    return whole


def layer(params, tokens, ids, out_grad):
    (w_qkv, w_out, w_in, w_back, vectors) = params
    n1_gain, n1_bias, q_bias, v_bias, o_bias, n2_gain, n2_bias, back_bias, in_bias = vectors
    resid_in = tokens.astype(F32)
    normal1, rstd1 = norm_stats(resid_in)
    normed1 = (normal1 * n1_gain + n1_bias).astype(BF)
    qkv_shift = jnp.concatenate([q_bias, jnp.zeros_like(q_bias), v_bias])
    qkv_rows = (times(normed1, w_qkv) + qkv_shift).astype(BF)
    attn, lse = attention(qkv_rows, ids)
    resid_mid = resid_in + times(attn, w_out) + o_bias
    normal2, rstd2 = norm_stats(resid_mid)
    normed2 = (normal2 * n2_gain + n2_bias).astype(BF)
    pre_act = times(normed2, w_in) + in_bias
    cdf = 0.5 * (1.0 + lax.erf(pre_act * 0.7071067811865476))
    hidden = (pre_act * cdf).astype(BF)
    block_out = (resid_mid + times(hidden, w_back) + back_bias).astype(BF)

    g_backb = jnp.sum(out_grad, axis=0, dtype=F32)
    g_wback = reduce_grad(inner_rows(hidden, out_grad))
    slope = cdf + pre_act * (0.3989422804014327 * jnp.exp(-0.5 * pre_act * pre_act))
    pre_grad = (times_trans(out_grad, w_back) * slope).astype(BF)
    g_inb = jnp.sum(pre_grad, axis=0, dtype=F32)
    g_win = reduce_grad(inner_rows(normed2, pre_grad))
    n2_grad = times_trans(pre_grad, w_in)
    g_n2g = jnp.sum(n2_grad * normal2, axis=0)
    g_n2b = jnp.sum(n2_grad, axis=0)
    mid_grad = out_grad.astype(F32) + norm_back(n2_grad, normal2, rstd2, n2_gain)
    branch = mid_grad.astype(BF)
    g_ob = jnp.sum(branch, axis=0, dtype=F32)
    g_wout = reduce_grad(inner_rows(attn, branch))
    attn_grad = times_trans(branch, w_out).astype(BF)
    qkv_grad = attention_back(qkv_rows, ids, attn, lse, attn_grad)
    g_qb = jnp.sum(qkv_grad[:, :D], axis=0, dtype=F32)
    g_vb = jnp.sum(qkv_grad[:, 2 * D :], axis=0, dtype=F32)
    g_qkv = reduce_grad(inner_rows(normed1, qkv_grad))
    n1_grad = times_trans(qkv_grad, w_qkv)
    g_n1g = jnp.sum(n1_grad * normal1, axis=0)
    g_n1b = jnp.sum(n1_grad, axis=0)
    token_grad = (mid_grad + norm_back(n1_grad, normal1, rstd1, n1_gain)).astype(BF)
    small = (g_n1g, g_n1b, g_qb, g_vb, g_ob, g_n2g, g_n2b, g_backb, g_inb)
    return block_out, token_grad, (g_qkv, g_wout, g_win, g_wback), small


def body(
    tokens,
    segment_ids,
    out_grad,
    norm1_gain,
    norm1_bias,
    qkv_weight,
    query_bias,
    value_bias,
    out_weight,
    out_bias,
    norm2_gain,
    norm2_bias,
    ff_in_weight,
    ff_in_bias,
    ff_out_weight,
    ff_out_bias,
):
    seqs, row_count, _ = tokens.shape
    ways = lax.axis_size("seq")
    me = lax.axis_index("seq")
    shards = lax.axis_size("shard")
    shard = lax.axis_index("shard")
    cell = norm1_gain.shape[0]

    vec = jnp.concatenate(
        [
            norm1_gain,
            norm1_bias,
            query_bias,
            value_bias,
            out_bias,
            norm2_gain,
            norm2_bias,
            ff_out_bias,
            ff_in_bias,
        ]
    )
    vec_all = lax.all_gather(vec, "shard", axis=0).astype(F32)
    w_qkv = lax.all_gather(qkv_weight, "shard", axis=0, tiled=True)
    w_out = lax.all_gather(out_weight, "shard", axis=0, tiled=True)
    w_in = lax.all_gather(ff_in_weight, "shard", axis=0, tiled=True)
    w_back = lax.all_gather(ff_out_weight, "shard", axis=0, tiled=True)
    vectors = [vec_all[:, i * cell : (i + 1) * cell].reshape(-1) for i in range(8)]
    vectors.append(vec_all[:, 8 * cell :].reshape(-1))
    params = (w_qkv, w_out, w_in, w_back, vectors)

    out_parts, grad_parts = [], []
    weight_totals, small_totals = None, None
    for group in range(seqs // ways):
        lo = group * ways
        rows = swap_halves(tokens[lo : lo + ways], me).reshape(ways * row_count, -1)
        cots = swap_halves(out_grad[lo : lo + ways], me).reshape(ways * row_count, -1)
        ids = pick(segment_ids[lo : lo + ways], me)
        block, tgrad, grads, small = layer(params, rows, ids, cots)
        out_parts.append(swap_halves(block.reshape(ways, row_count, -1), me))
        grad_parts.append(swap_halves(tgrad.reshape(ways, row_count, -1), me))
        if group == 0:
            weight_totals, small_totals = grads, small
        else:
            weight_totals = jax.tree.map(jnp.add, weight_totals, grads)
            small_totals = jax.tree.map(jnp.add, small_totals, small)
    g_qkv, g_wout, g_win, g_wback = weight_totals
    packed = jnp.concatenate([s.reshape(shards, -1) for s in small_totals], axis=1)
    mine = pick(sum_all(packed), shard)
    s = [mine[i * cell : (i + 1) * cell] for i in range(8)] + [mine[8 * cell :]]
    return (
        jnp.concatenate(out_parts, axis=0),
        jnp.concatenate(grad_parts, axis=0),
        s[0],
        s[1],
        g_qkv,
        s[2],
        s[3],
        g_wout,
        s[4],
        s[5],
        s[6],
        g_win,
        s[8],
        g_wback,
        s[7],
    )


def solution(mesh):
    in_specs = (
        P(("shard", "rep"), "seq", None),
        P(("shard", "rep"), None),
        P(("shard", "rep"), "seq", None),
        P("shard"),
        P("shard"),
        P("shard", None),
        P("shard"),
        P("shard"),
        P("shard", None),
        P("shard"),
        P("shard"),
        P("shard"),
        P("shard", None),
        P("shard"),
        P("shard", None),
        P("shard"),
    )
    out_specs = (
        P(("shard", "rep"), "seq", None),
        P(("shard", "rep"), "seq", None),
        P("shard"),
        P("shard"),
        P("shard", None),
        P("shard"),
        P("shard"),
        P("shard", None),
        P("shard"),
        P("shard"),
        P("shard"),
        P("shard", None),
        P("shard"),
        P("shard", None),
        P("shard"),
    )
    return jax.shard_map(body, mesh=mesh, in_specs=in_specs, out_specs=out_specs, check_vma=False)
```

time: 1060 us -> 584 us (0.55)
  waiting for transfers between devices: 549 us -> 124 us
  matrix products: 274 us -> 198 us
  starting transfers between devices: 1.31 us -> 70.8 us
  blocking collectives: 71.2 us -> 5.2 us
  other arithmetic: 52.6 us -> 79.6 us
  local copies, waits for them, and re-layouts: 93.7 us -> 83.1 us
    reduce_scatter x6 -> x0, waiting for transfers between devices: 321 us -> none  [the longest x4 254 us: body(): owned = lax.psum_scatter(totals, 'shard', scatter_dimension=0, tiled=True)]
    psum x1 -> x0, waiting for transfers between devices: 160 us -> none  [body(): summed = lax.psum(owned, ('seq', 'rep'))]
    ppermute x0 -> x49, waiting for transfers between devices: none -> 122 us  [xor_send(): return lax.ppermute(value, axis, [(i, i ^ mask) for i in range(size)])]
    ppermute x0 -> x49, starting transfers between devices: none -> 70.7 us  [xor_send(): return lax.ppermute(value, axis, [(i, i ^ mask) for i in range(size)])]
    all_gather x6 -> x4, waiting for transfers between devices: 65.6 us -> 0.04 us  [the longest x1 0.02 us: body(): w_in = lax.all_gather(ff_in_weight, 'shard', axis=0, tiled=True)]
    sub x6 -> x0, matrix products: 54.9 us -> none  [forward_pass(): expo = jnp.exp(scores - top_val)]
    psum x1 -> x0, blocking collectives: 39.8 us -> none  [body(): summed = lax.psum(owned, ('seq', 'rep'))]
    unnamed x392 -> x216, local copies, waits for them, and re-layouts: 49.1 us -> 17.8 us
  transfers between devices with their start and end apart: 13 -> 53, of which waited for: 9 -> 25; matrix products, arithmetic and copies ran while one was open for 27% -> 34% of each run, Pallas kernels for 0% -> 0%
where the time goes in v1:
time: 584 us; the launch traced here: 576 us
  matrix products  198 us (34%)
  waiting for transfers between devices  124 us (21%)
  local copies, waits for them, and re-layouts  83.1 us (14%)
  other arithmetic  79.6 us (14%)
  starting transfers between devices  70.8 us (12%)
  between operations  15.8 us (3%)
    ppermute x49, waiting for transfers between devices, xor_send(): return lax.ppermute(value, axis, [(i, i ^ mask) for i in range(size)])  122 us
    ppermute x49, starting transfers between devices, xor_send(): return lax.ppermute(value, axis, [(i, i ^ mask) for i in range(size)])  70.7 us
    convert_element_type x3, other arithmetic, attention_back(): score_grad = (probs * (prob_grad - row_inner)).astype(BF)  32.9 us
    dot_general x4, matrix products, times(): return jnp.dot(left, right, preferred_element_type=jnp.float32)  32.6 us
    dot_general x4, matrix products, times_trans(): lax.dot_general(left, right, (((1,), (1,)), ((), ())), preferred_element_...  31.1 us
    dot_general x4, matrix products, inner_rows(): lax.dot_general(left, right, (((0,), (0,)), ((), ())), preferred_element_...  26.3 us
    dot_general x3, matrix products, head_scores(): jnp.einsum('qhd,khd->hqk', query_grp, key_grp, preferred_element_type=jnp...  26.1 us
    dot_general x3, matrix products, attention_back(): jnp.einsum('qhd,khd->hqk', attn_grp, value_grp, preferred_element_type=F32)  25.6 us
  transfers between devices with their start and end apart: 53, of which 25 were waited for; matrix products, arithmetic and copies ran while one was open for 34% of the time, Pallas kernels for 0%

profile of v1, /device:TPU:0, one launch (start us, length us, event | category | flops | bytes accessed | tf_op | source)
XLA Modules:
  0.0 576.3 jit_solution(11976277256695566937)
XLA Ops:
  15.4 5.2 all-gather.1
  22.7 9.7 %collective-permute-done.2 = bf16[512,768]{1,0:T(8,128)(2,1)} collective-permute-done((bf16[512,768]{1,0:T(8,128)(2,1)}, bf16[512,768]{1,0:T(8,128)(2,1)}, u32[]{:S(2)}, u32[]{:S(2)}) %collective-permute-start.2) | collective-permute-done | bytes 786464 | tf_op jit(solution)/shard_map/ppermute | solution.py:16
  36.8 11.5 %collective-permute-done = bf16[512,768]{1,0:T(8,128)(2,1)S(1)} collective-permute-done((bf16[512,768]{1,0:T(8,128)(2,1)}, bf16[512,768]{1,0:T(8,128)(2,1)S(1)}, u32[]{:S(2)}, u32[]{:S(2)}) %collective-permute-start) | collective-permute-done | bytes 786464 | tf_op jit(solution)/shard_map/ppermute | solution.py:16
  54.1 6.3 %add_convert_fusion = bf16[1024,2304]{1,0:T(8,128)(2,1)S(1)} fusion(bf16[1024,768]{1,0:T(8,128)(2,1)} %fusion.40, bf16[768,2304]{1,0:T(8,128)(2,1)} %all-gather.7.cloned.1.call-done, f32[2304]{0:T(1024)S(1)} %pad_maximum_fusion.3), kind=kOutput, calls=%fused_computation.40 | convolution fusion | flops 3628597248 | bytes 9839616 | tf_op jit(solution)/shard_map/dot_general | solution.py:107
  79.3 10.0 %fusion.117 = (f32[4,1024]{1,0:T(4,128)S(1)}, f32[4,1024,1024]{1,2,0:T(8,128)}) fusion(bf16[1024,4,64]{0,2,1:T(8,128)(2,1)} %bitcast.319, bf16[1024,4,64]{0,2,1:T(8,128)(2,1)} %bitcast.317, pred[1024,1024]{0,1:T(8,128)(4,1)S(1)} %broadcast_compare_fusion), kind=kOutput, calls=%fused_computation.257 | convolution fusion | flops 549449728 | bytes 18890752 | tf_op jit(solution)/shard_map/qhd,khd->hqk/dot_general | solution.py:111
  89.4 8.2 %fusion = f32[4,1024]{1,0:T(4,128)S(1)} fusion(f32[4,1024,1024]{1,2,0:T(8,128)} %get-tuple-element.88, f32[4,1024]{1,0:T(4,128)S(1)} %get-tuple-element.87), kind=kLoop, calls=%fused_computation.19 | loop fusion | flops 8384512 | bytes 16809984 | tf_op jit(solution)/shard_map/reduce_sum | solution.py:131
  97.5 8.4 %fusion.68 = bf16[4,64,1024]{2,1,0:T(8,128)(2,1)} fusion(bf16[1024,4,64]{0,2,1:T(8,128)(2,1)S(1)} %bitcast.354, f32[4,1024,1024]{1,2,0:T(8,128)} %get-tuple-element.88, f32[4,1024]{1,0:T(4,128)S(1)} %fusion, f32[4,1024]{1,0:T(4,128)S(1)} %get-tuple-element.87), kind=kOutput, calls=%fused_computation.122 | convolution fusion | flops 549715968 | bytes 17858560 | tf_op jit(solution)/shard_map/hqk,khd->qhd/dot_general | solution.py:133
  106.0 8.5 %fusion.116 = (f32[4,1024]{1,0:T(4,128)S(1)}, f32[4,1024,1024]{1,2,0:T(8,128)}) fusion(bf16[1024,4,64]{0,2,1:T(8,128)(2,1)S(1)} %bitcast.311, bf16[1024,4,64]{0,2,1:T(8,128)(2,1)S(1)} %bitcast.309, pred[1024,1024]{0,1:T(8,128)(4,1)S(1)} %broadcast_compare_fusion), kind=kOutput, calls=%fused_computation.256 | convolution fusion | flops 549449728 | bytes 18890752 | tf_op jit(solution)/shard_map/qhd,khd->hqk/dot_general | solution.py:111
  114.5 8.1 %fusion.1 = f32[4,1024]{1,0:T(4,128)S(1)} fusion(f32[4,1024,1024]{1,2,0:T(8,128)} %get-tuple-element.86, f32[4,1024]{1,0:T(4,128)S(1)} %get-tuple-element.85), kind=kLoop, calls=%fused_computation.20 | loop fusion | flops 8384512 | bytes 16809984 | tf_op jit(solution)/shard_map/reduce_sum | solution.py:131
  122.6 7.5 %fusion.115 = (f32[4,1024]{1,0:T(4,128)S(1)}, f32[4,1024,1024]{1,2,0:T(8,128)}) fusion(bf16[1024,4,64]{0,2,1:T(8,128)(2,1)S(1)} %bitcast.315, bf16[1024,4,64]{0,2,1:T(8,128)(2,1)S(1)} %bitcast.313, pred[1024,1024]{0,1:T(8,128)(4,1)S(1)} %broadcast_compare_fusion), kind=kOutput, calls=%fused_computation.255 | convolution fusion | flops 549449728 | bytes 18890752 | tf_op jit(solution)/shard_map/qhd,khd->hqk/dot_general | solution.py:111
  130.2 8.2 %fusion.2 = f32[4,1024]{1,0:T(4,128)S(1)} fusion(f32[4,1024,1024]{1,2,0:T(8,128)} %get-tuple-element.84, f32[4,1024]{1,0:T(4,128)S(1)} %get-tuple-element.83), kind=kLoop, calls=%fused_computation.21 | loop fusion | flops 8384512 | bytes 16809984 | tf_op jit(solution)/shard_map/reduce_sum | solution.py:131
  138.5 8.4 %fusion.67 = bf16[4,64,1024]{2,1,0:T(8,128)(2,1)} fusion(bf16[1024,4,64]{0,2,1:T(8,128)(2,1)S(1)} %bitcast.350, f32[4,1024,1024]{1,2,0:T(8,128)} %get-tuple-element.86, f32[4,1024]{1,0:T(4,128)S(1)} %fusion.1, f32[4,1024]{1,0:T(4,128)S(1)} %get-tuple-element.85), kind=kOutput, calls=%fused_computation.121 | convolution fusion | flops 549715968 | bytes 17858560 | tf_op jit(solution)/shard_map/hqk,khd->qhd/dot_general | solution.py:133
  148.1 4.2 fusion.66
  157.8 12.8 %fusion.15 = (bf16[3072,1024]{0,1:T(8,128)(2,1)}, f32[1024,3072]{1,0:T(8,128)}) fusion(f32[3072]{0:T(1024)S(1)} %add.396, bf16[768,3072]{1,0:T(8,128)(2,1)} %all-gather.11.cloned.1.call-done, f32[1024,768]{1,0:T(8,128)} %copy-done.4, f32[768]{0:T(1024)S(1)} %add.393, f32[768]{0:T(1024)S(1)} %mul.270, f32[1024]{0:T(1024)S(1)} %add_rsqrt_fusion, ...), kind=kOutput, calls=%fused_computation.39 | convolution fusion | flops 4854644736 | bytes 26765312 | tf_op jit(solution)/shard_map/dot_general | solution.py:107
  170.6 11.9 %convert_reduce_fusion = (f32[3072]{0:T(1024)S(1)}, bf16[1024,3072]{1,0:T(8,128)(2,1)S(1)}) fusion(f32[1024,3072]{1,0:T(8,128)} %get-tuple-element.102, f32[3072]{0:T(1024)S(1)} %add.396, bf16[1024,768]{1,0:T(8,128)(2,1)S(1)} %bitcast.303, bf16[3072,768]{1,0:T(8,128)(2,1)} %all-gather.13.cloned.1.call-done), kind=kOutput, calls=%fused_computation.36 | convolution fusion | flops 4872729600 | bytes 25190400 | tf_op jit(solution)/shard_map/dot_general | solution.py:101
  185.2 8.4 %fusion.105 = f32[768,3072]{1,0:T(8,128)} fusion(bf16[1024,3072]{1,0:T(8,128)(2,1)S(1)} %get-tuple-element.100, f32[1024,768]{1,0:T(8,128)S(1)} %copy-done.5, f32[768]{0:T(1024)S(1)} %add.393, f32[768]{0:T(1024)S(1)} %mul.270, f32[1024]{0:T(1024)S(1)} %add_rsqrt_fusion, f32[1024]{0:T(1024)S(1)} %broadcast_multiply_fusion.4), kind=kOutput, calls=%fused_computation.249 | convolution fusion | flops 4835770368 | bytes 18888704 | tf_op jit(solution)/shard_map/dot_general | solution.py:95
  193.6 9.3 %multiply_reduce_fusion.3 = (f32[768]{0:T(1024)S(1)}, f32[1024]{0:T(1024)S(1)}, f32[1024]{0:T(1024)S(1)}, f32[768]{0:T(1024)S(1)}, f32[1024,768]{1,0:T(8,128)}) fusion(f32[1024,768]{1,0:T(8,128)S(1)} %copy-done.5, f32[1024]{0:T(1024)S(1)} %add_rsqrt_fusion, f32[1024]{0:T(1024)S(1)} %broadcast_multiply_fusion.4, f32[768]{0:T(1024)S(1)} %mul.270, ...), kind=kOutput, calls=%fused_computation.81 | convolution fusion | flops 4838912000 | bytes 17327104 | tf_op jit(solution)/shard_map/dot_general | solution.py:101
  212.5 8.5 %fusion.57 = bf16[4,64,1024]{2,1,0:T(8,128)(2,1)S(1)} fusion(bf16[1024,4,64]{0,2,1:T(8,128)(2,1)S(1)} %bitcast.328, f32[4,1024,1024]{1,2,0:T(8,128)} %get-tuple-element.84, f32[4,1024]{1,0:T(4,128)S(1)} %log_add_fusion), kind=kOutput, calls=%fused_computation.113 | convolution fusion | flops 545521664 | bytes 17842176 | tf_op jit(solution)/shard_map/hqk,qhd->khd/dot_general | solution.py:153
  222.0 8.8 %fusion.51 = bf16[4,64,1024]{2,1,0:T(8,128)(2,1)S(1)} fusion(bf16[1024,4,64]{0,2,1:T(8,128)(2,1)} %bitcast.330, f32[4,1024,1024]{1,2,0:T(8,128)} %get-tuple-element.88, f32[4,1024]{1,0:T(4,128)S(1)} %log_add_fusion.2), kind=kOutput, calls=%fused_computation.111 | convolution fusion | flops 545521664 | bytes 17842176 | tf_op jit(solution)/shard_map/hqk,qhd->khd/dot_general | solution.py:153
  233.9 4.3 fusion.69
  238.1 10.7 %multiply_reduce_fusion.2 = (f32[4,1024]{1,0:T(4,128)S(1)}, f32[4,1024,1024]{1,2,0:T(8,128)}) fusion(f32[4,1024,1024]{1,2,0:T(8,128)} %get-tuple-element.88, f32[4,1024]{1,0:T(4,128)S(1)} %log_add_fusion.2, bf16[1024,4,64]{0,2,1:T(8,128)(2,1)S(1)} %bitcast.331, bf16[1024,4,64]{0,2,1:T(8,128)(2,1)S(1)} %bitcast.355), kind=kOutput, calls=%fused_computation.8 | convolution fusion | flops 549449728 | bytes 34635776 | tf_op jit(solution)/shard_map/qhd,khd->hqk/dot_general | solution.py:154
  248.9 12.5 %multiply_convert_fusion.2 = bf16[4,1024,1024]{1,2,0:T(8,128)(2,1)S(1)} fusion(f32[4,1024,1024]{1,2,0:T(8,128)} %get-tuple-element.93, f32[4,1024,1024]{1,2,0:T(8,128)} %get-tuple-element.88, f32[4,1024]{1,0:T(4,128)S(1)} %get-tuple-element.92, f32[4,1024]{1,0:T(4,128)S(1)} %log_add_fusion.2), kind=kLoop, calls=%fused_computation.7 | loop fusion | flops 16777216 | bytes 41975808 | tf_op jit(solution)/shard_map/convert_element_type | solution.py:156
  261.4 3.5 fusion.63
  266.5 7.4 %multiply_reduce_fusion = (f32[4,1024]{1,0:T(4,128)S(1)}, f32[4,1024,1024]{1,2,0:T(8,128)}) fusion(f32[4,1024,1024]{1,2,0:T(8,128)S(1)} %bitcast.298, f32[4,1024]{1,0:T(4,128)S(1)} %log_add_fusion, bf16[1024,4,64]{0,2,1:T(8,128)(2,1)S(1)} %bitcast.329, bf16[1024,4,64]{0,2,1:T(8,128)(2,1)S(1)} %bitcast.353), kind=kOutput, calls=%fused_computation.2 | convolution fusion | flops 549449728 | bytes 34635776 | tf_op jit(solution)/shard_map/qhd,khd->hqk/dot_general | solution.py:154
  274.0 12.1 %multiply_convert_fusion = bf16[4,1024,1024]{1,2,0:T(8,128)(2,1)S(1)} fusion(f32[4,1024,1024]{1,2,0:T(8,128)} %get-tuple-element.97, f32[4,1024,1024]{1,2,0:T(8,128)} %get-tuple-element.84, f32[4,1024]{1,0:T(4,128)S(1)} %get-tuple-element.96, f32[4,1024]{1,0:T(4,128)S(1)} %log_add_fusion), kind=kLoop, calls=%fused_computation.1 | loop fusion | flops 16777216 | bytes 41975808 | tf_op jit(solution)/shard_map/convert_element_type | solution.py:156
  286.1 3.5 fusion.65
  291.2 7.4 %multiply_reduce_fusion.1 = (f32[4,1024]{1,0:T(4,128)S(1)}, f32[4,1024,1024]{1,2,0:T(8,128)}) fusion(f32[4,1024,1024]{1,2,0:T(8,128)S(1)} %bitcast.294, f32[4,1024]{1,0:T(4,128)S(1)} %log_add_fusion.1, bf16[1024,4,64]{0,2,1:T(8,128)(2,1)S(1)} %bitcast.327, bf16[1024,4,64]{0,2,1:T(8,128)(2,1)S(1)} %bitcast.351), kind=kOutput, calls=%fused_computation.5 | convolution fusion | flops 549449728 | bytes 34635776 | tf_op jit(solution)/shard_map/qhd,khd->hqk/dot_general | solution.py:154
  298.7 8.3 %multiply_convert_fusion.1 = bf16[4,1024,1024]{1,2,0:T(8,128)(2,1)S(1)} fusion(f32[4,1024,1024]{1,2,0:T(8,128)} %get-tuple-element.95, f32[4,1024,1024]{1,2,0:T(8,128)S(1)} %bitcast.294, f32[4,1024]{1,0:T(4,128)S(1)} %get-tuple-element.94, f32[4,1024]{1,0:T(4,128)S(1)} %log_add_fusion.1), kind=kLoop, calls=%fused_computation.4 | loop fusion | flops 16777216 | bytes 41975808 | tf_op jit(solution)/shard_map/convert_element_type | solution.py:156
  307.0 3.5 fusion.64
  315.3 8.9 %copy.150 = bf16[3072,1024]{1,0:T(8,128)(2,1)} copy(bf16[3072,1024]{0,1:T(8,128)(2,1)} %get-tuple-element.101) | data formatting | bytes 12582912 | tf_op jit(solution)/shard_map/dot_general | solution.py:95
  326.6 10.3 %add_convert_fusion.1 = bf16[1024,768]{1,0:T(8,128)(2,1)S(1)} fusion(f32[1024,768]{1,0:T(8,128)S(1)} %copy-done.6, bf16[3072,768]{1,0:T(8,128)(2,1)} %all-gather.13.cloned.1.call-done, f32[1024,3072]{1,0:T(8,128)} %get-tuple-element.102, f32[3072]{0:T(1024)S(1)} %add.396, f32[768]{0:T(1024)S(1)} %copy-done.69), kind=kOutput, calls=%fused_computation.87 | convolution fusion | flops 4853071872 | bytes 22035456 | tf_op jit(solution)/shard_map/dot_general | solution.py:107
  339.9 4.2 fusion.48
  356.6 8.4 %fusion.46 = (f32[768]{0:T(1024)S(1)}, f32[1024]{0:T(1024)S(1)}, f32[1024]{0:T(1024)S(1)}, f32[768]{0:T(1024)S(1)}, f32[1024,768]{1,0:T(8,128)}) fusion(bf16[2,512,768]{2,1,0:T(8,128)(2,1)S(1)} %copy-done.3, f32[1024]{0:T(1024)S(1)} %bitcast.373, f32[1024]{0:T(1024)S(1)} %bitcast.370, f32[768]{0:T(1024)S(1)} %copy-done.63, ...), kind=kOutput, calls=%fused_computation.78 | convolution fusion | flops 3631739392 | bytes 13001728 | tf_op jit(solution)/shard_map/dot_general | solution.py:101
  365.6 6.2 %fusion.30 = f32[2,2,192,2304]{3,2,1,0:T(8,128)S(1)} fusion(bf16[2,2,192,1024]{3,2,1,0:T(8,128)(2,1)S(1)} %bitcast.361, bf16[1024,2304]{1,0:T(8,128)(2,1)} %constant_dynamic-update-slice_fusion.24), kind=kOutput, calls=%fused_computation.52 | convolution fusion | flops 3623878656 | bytes 13369344 | tf_op jit(solution)/shard_map/dot_general | solution.py:95
  373.2 7.4 %fusion.119 = f32[2,2,768,768]{3,2,1,0:T(8,128)S(1)} fusion(bf16[2,2,768,1024]{3,2,1,0:T(8,128)(2,1)} %bitcast.321, bf16[1024,768,1,1]{1,0,3,2:T(8,128)(2,1)S(1)} %bitcast.304), kind=kOutput, calls=%fused_computation.259 | convolution fusion | flops 4831838208 | bytes 17301504 | tf_op jit(solution)/shard_map/dot_general | solution.py:95
  398.6 5.0 collective-permute-done.20
  432.5 3.9 collective-permute-done.27
  437.2 4.4 collective-permute-done.28
  446.5 6.9 %collective-permute-done.11 = bf16[96,2304]{1,0:T(8,128)(2,1)S(1)} collective-permute-done((bf16[96,2304]{1,0:T(8,128)(2,1)S(1)}, bf16[96,2304]{1,0:T(8,128)(2,1)S(1)}, u32[]{:S(2)}, u32[]{:S(2)}) %collective-permute-start.11) | collective-permute-done | bytes 442400 | tf_op jit(solution)/shard_map/ppermute | solution.py:16
  471.8 5.7 collective-permute-done.16
  480.2 15.8 %collective-permute-done.40 = bf16[1,768,768]{2,1,0:T(8,128)(2,1)S(1)} collective-permute-done((bf16[1,768,768]{2,1,0:T(8,128)(2,1)S(1)}, bf16[1,768,768]{2,1,0:T(8,128)(2,1)S(1)}, u32[]{:S(2)}, u32[]{:S(2)}) %collective-permute-start.40) | collective-permute-done | bytes 1179680 | tf_op jit(solution)/shard_map/ppermute | solution.py:16
  508.0 3.9 collective-permute-done.41
  512.0 3.4 collective-permute-start.42
  521.6 6.0 %collective-permute-start.37 = (bf16[24,3072]{1,0:T(8,128)(2,1)S(1)}, bf16[24,3072]{1,0:T(8,128)(2,1)S(1)}, u32[]{:S(2)}, u32[]{:S(2)}) collective-permute-start(bf16[24,3072]{1,0:T(8,128)(2,1)S(1)} %get-tuple-element.26), channel_id=1, source_target_pairs={{0,3},{1,2},{2,1},{3,0},{4,7},{5,6},{6,5},{7,4},{8,11},{9,10},{10,... | collective-permute-start | bytes 442376 | tf_op jit(solution)/shard_map/ppermute | solution.py:16
  527.6 11.4 %collective-permute-done.43 = bf16[96,768]{1,0:T(8,128)(2,1)S(1)} collective-permute-done((bf16[96,768]{1,0:T(8,128)(2,1)S(1)}, bf16[96,768]{1,0:T(8,128)(2,1)S(1)}, u32[]{:S(2)}, u32[]{:S(2)}) %collective-permute-start.43) | collective-permute-done | bytes 147488 | tf_op jit(solution)/shard_map/ppermute | solution.py:16
  546.1 7.1 %collective-permute-done.46 = bf16[96,768]{1,0:T(8,128)(2,1)S(1)} collective-permute-done((bf16[96,768]{1,0:T(8,128)(2,1)S(1)}, bf16[96,768]{1,0:T(8,128)(2,1)S(1)}, u32[]{:S(2)}, u32[]{:S(2)}) %collective-permute-start.46) | collective-permute-done | bytes 147488 | tf_op jit(solution)/shard_map/ppermute | solution.py:16
  554.3 3.3 collective-permute-done.38
  559.3 8.7 %collective-permute-done.48 = bf16[384,768]{1,0:T(8,128)(2,1)S(1)} collective-permute-done((bf16[384,768]{1,0:T(8,128)(2,1)S(1)}, bf16[384,768]{1,0:T(8,128)(2,1)S(1)}, u32[]{:S(2)}, u32[]{:S(2)}) %collective-permute-start.48) | collective-permute-done | bytes 589856 | tf_op jit(solution)/shard_map/ppermute | solution.py:16
  (471 shorter events, 192.7 us)
Async XLA Ops:
  7.2 46.8 %all-gather.7.cloned.1.call-start = ((), (), s32[]{:S(2)}) async-start(), calls=%async_computation | async-start | bytes 4423680 | tf_op jit(solution)/shard_map/all_gather | solution.py:258
  7.9 144.4 %all-gather.9.cloned.1.call-start = ((), (), s32[]{:S(2)}) async-start(), calls=%async_computation.1 | async-start | bytes 1474560 | tf_op jit(solution)/shard_map/all_gather | solution.py:259
  8.7 149.1 %all-gather.11.cloned.1.call-start = ((), (), s32[]{:S(2)}) async-start(), calls=%async_computation.2 | async-start | bytes 5898240 | tf_op jit(solution)/shard_map/all_gather | solution.py:260
  9.4 161.2 %all-gather.13.cloned.1.call-start = ((), (), s32[]{:S(2)}) async-start(), calls=%async_computation.3 | async-start | bytes 5898240 | tf_op jit(solution)/shard_map/all_gather | solution.py:261
  10.7 21.7 %collective-permute-start.2 = (bf16[512,768]{1,0:T(8,128)(2,1)}, bf16[512,768]{1,0:T(8,128)(2,1)}, u32[]{:S(2)}, u32[]{:S(2)}) collective-permute-start(bf16[512,768]{1,0:T(8,128)(2,1)} %get-tuple-element.47), channel_id=1, source_target_pairs={{0,16},{16,0},{1,17},{17,1},{2,18},{18,2},{3,19},{19,3},{4,20},{20... | collective-permute-start | bytes 2359304 | tf_op jit(solution)/shard_map/ppermute | solution.py:16
  14.9 33.5 %collective-permute-start = (bf16[512,768]{1,0:T(8,128)(2,1)}, bf16[512,768]{1,0:T(8,128)(2,1)S(1)}, u32[]{:S(2)}, u32[]{:S(2)}) collective-permute-start(bf16[512,768]{1,0:T(8,128)(2,1)} %get-tuple-element.51), channel_id=1, source_target_pairs={{0,16},{16,0},{1,17},{17,1},{2,18},{18,2},{3,19},{19,3},{4,20},{20... | collective-permute-start | bytes 2359304 | tf_op jit(solution)/shard_map/ppermute | solution.py:16
  326.6 68.7 %collective-permute-start.19 = (bf16[2,192,768]{2,1,0:T(8,128)(2,1)}, bf16[2,192,768]{2,1,0:T(8,128)(2,1)}, u32[]{:S(2)}, u32[]{:S(2)}) collective-permute-start(bf16[2,192,768]{2,1,0:T(8,128)(2,1)} %fusion.70), channel_id=1, source_target_pairs={{0,4},{4,0},{8,12},{12,8},{1,5},{5,1},{9,13},{13,9},{2,6},{6,2},{1... | collective-permute-start | bytes 1769480 | tf_op jit(solution)/shard_map/ppermute | solution.py:16
  338.1 84.0 %collective-permute-start.1 = (bf16[512,768]{1,0:T(8,128)(2,1)}, bf16[512,768]{1,0:T(8,128)(2,1)}, u32[]{:S(2)}, u32[]{:S(2)}) collective-permute-start(bf16[512,768]{1,0:T(8,128)(2,1)} %get-tuple-element.49), channel_id=1, source_target_pairs={{0,16},{16,0},{1,17},{17,1},{2,18},{18,2},{3,19},{19,3},{4,20},{20... | collective-permute-start | bytes 2359304 | tf_op jit(solution)/shard_map/ppermute | solution.py:16
  365.3 15.3 %collective-permute-start.4 = (f32[4,2304]{1,0:T(4,128)S(1)}, f32[4,2304]{1,0:T(4,128)S(1)}, u32[]{:S(2)}, u32[]{:S(2)}) collective-permute-start(f32[4,2304]{1,0:T(4,128)S(1)} %concatenate.29), channel_id=1, source_target_pairs={{0,4},{4,0},{8,12},{12,8},{1,5},{5,1},{9,13},{13,9},{2,6},{6,2},{1... | collective-permute-start | bytes 110600 | tf_op jit(solution)/shard_map/ppermute | solution.py:16
  383.8 33.9 %collective-permute-start.9 = (bf16[2,192,2304]{2,1,0:T(8,128)(2,1)S(1)}, bf16[2,192,2304]{2,1,0:T(8,128)(2,1)S(1)}, u32[]{:S(2)}, u32[]{:S(2)}) collective-permute-start(bf16[2,192,2304]{2,1,0:T(8,128)(2,1)S(1)} %fusion.50), channel_id=1, source_target_pairs={{0,4},{4,0},{8,12},{12,8},{1,5},{5,1},{9,13},{13,9},{2,6},{6,2},{1... | collective-permute-start | bytes 5308424 | tf_op jit(solution)/shard_map/ppermute | solution.py:16
  392.7 5.8 %collective-permute-start.8 = (f32[4,2304]{1,0:T(4,128)S(1)}, f32[4,2304]{1,0:T(4,128)S(1)}, u32[]{:S(2)}, u32[]{:S(2)}) collective-permute-start(f32[4,2304]{1,0:T(4,128)S(1)} %add.414), channel_id=1, source_target_pairs={{0,2},{1,3},{2,0},{3,1},{4,6},{5,7},{6,4},{7,5},{8,10},{9,11},{10,... | collective-permute-start | bytes 110600 | tf_op jit(solution)/shard_map/ppermute | solution.py:16
  396.8 6.8 %collective-permute-start.20 = (bf16[1,192,768]{2,1,0:T(8,128)(2,1)S(1)}, bf16[1,192,768]{2,1,0:T(8,128)(2,1)S(1)}, u32[]{:S(2)}, u32[]{:S(2)}) collective-permute-start(bf16[1,192,768]{2,1,0:T(8,128)(2,1)S(1)} %dynamic-slice_convert_fusion.10), channel_id=1, source_target_pairs={{0,8},{4,12},{8,0},{12,4},{1,9},{5,13},{9,1},{13,5},{2,10},{6,14},... | collective-permute-start | bytes 884744 | tf_op jit(solution)/shard_map/ppermute | solution.py:16
  403.6 5.2 collective-permute-start.21
  410.5 5.8 collective-permute-start.24
  410.9 5.4 collective-permute-start.23
  413.1 30.7 %collective-permute-start.29 = (bf16[2,192,3072]{2,1,0:T(8,128)(2,1)S(1)}, bf16[2,192,3072]{2,1,0:T(8,128)(2,1)S(1)}, u32[]{:S(2)}, u32[]{:S(2)}) collective-permute-start(bf16[2,192,3072]{2,1,0:T(8,128)(2,1)S(1)} %copy-done.35), channel_id=1, source_target_pairs={{0,4},{4,0},{8,12},{12,8},{1,5},{5,1},{9,13},{13,9},{2,6},{6,2},{1... | collective-permute-start | bytes 7077896 | tf_op jit(solution)/shard_map/ppermute | solution.py:16
  416.2 41.2 %collective-permute-start.39 = (bf16[2,768,768]{2,1,0:T(8,128)(2,1)}, bf16[2,768,768]{2,1,0:T(8,128)(2,1)S(1)}, u32[]{:S(2)}, u32[]{:S(2)}) collective-permute-start(bf16[2,768,768]{2,1,0:T(8,128)(2,1)} %fusion.49), channel_id=1, source_target_pairs={{0,4},{4,0},{8,12},{12,8},{1,5},{5,1},{9,13},{13,9},{2,6},{6,2},{1... | collective-permute-start | bytes 7077896 | tf_op jit(solution)/shard_map/ppermute | solution.py:16
  416.2 20.8 %collective-permute-start.3 = (bf16[512,768]{1,0:T(8,128)(2,1)}, bf16[512,768]{1,0:T(8,128)(2,1)S(1)}, u32[]{:S(2)}, u32[]{:S(2)}) collective-permute-start(bf16[512,768]{1,0:T(8,128)(2,1)} %get-tuple-element.42), channel_id=1, source_target_pairs={{0,16},{16,0},{1,17},{17,1},{2,18},{18,2},{3,19},{19,3},{4,20},{20... | collective-permute-start | bytes 2359304 | tf_op jit(solution)/shard_map/ppermute | solution.py:16
  418.9 6.9 %collective-permute-start.25 = (bf16[24,768]{1,0:T(8,128)(2,1)S(1)}, bf16[24,768]{1,0:T(8,128)(2,1)S(1)}, u32[]{:S(2)}, u32[]{:S(2)}) collective-permute-start(bf16[24,768]{1,0:T(8,128)(2,1)S(1)} %get-tuple-element.28), channel_id=1, source_target_pairs={{0,1},{1,0},{2,3},{3,2},{4,5},{5,4},{6,7},{7,6},{8,9},{9,8},{10,11... | collective-permute-start | bytes 110600 | tf_op jit(solution)/shard_map/ppermute | solution.py:16
  422.1 20.7 %collective-permute-start.10 = (bf16[1,192,2304]{2,1,0:T(8,128)(2,1)S(1)}, bf16[1,192,2304]{2,1,0:T(8,128)(2,1)S(1)}, u32[]{:S(2)}, u32[]{:S(2)}) collective-permute-start(bf16[1,192,2304]{2,1,0:T(8,128)(2,1)S(1)} %dynamic-slice_convert_fusion.5), channel_id=1, source_target_pairs={{0,8},{4,12},{8,0},{12,4},{1,9},{5,13},{9,1},{13,5},{2,10},{6,14},... | collective-permute-start | bytes 2654216 | tf_op jit(solution)/shard_map/ppermute | solution.py:16
  430.7 5.8 collective-permute-start.27
  436.5 5.1 collective-permute-start.28
  443.1 10.3 %collective-permute-start.11 = (bf16[96,2304]{1,0:T(8,128)(2,1)S(1)}, bf16[96,2304]{1,0:T(8,128)(2,1)S(1)}, u32[]{:S(2)}, u32[]{:S(2)}) collective-permute-start(bf16[96,2304]{1,0:T(8,128)(2,1)S(1)} %fusion.73), channel_id=1, source_target_pairs={{0,16},{16,0},{1,17},{17,1},{2,18},{18,2},{3,19},{19,3},{4,20},{20... | collective-permute-start | bytes 1327112 | tf_op jit(solution)/shard_map/ppermute | solution.py:16
  444.9 33.4 %collective-permute-start.30 = (bf16[1,192,3072]{2,1,0:T(8,128)(2,1)S(1)}, bf16[1,192,3072]{2,1,0:T(8,128)(2,1)S(1)}, u32[]{:S(2)}, u32[]{:S(2)}) collective-permute-start(bf16[1,192,3072]{2,1,0:T(8,128)(2,1)S(1)} %dynamic-slice_convert_fusion.4), channel_id=1, source_target_pairs={{0,8},{4,12},{8,0},{12,4},{1,9},{5,13},{9,1},{13,5},{2,10},{6,14},... | collective-permute-start | bytes 3538952 | tf_op jit(solution)/shard_map/ppermute | solution.py:16
  453.5 6.9 %collective-permute-start.12 = (bf16[24,2304]{1,0:T(8,128)(2,1)S(1)}, bf16[24,2304]{1,0:T(8,128)(2,1)S(1)}, u32[]{:S(2)}, u32[]{:S(2)}) collective-permute-start(bf16[24,2304]{1,0:T(8,128)(2,1)S(1)} %get-tuple-element.59), channel_id=1, source_target_pairs={{0,1},{1,0},{2,3},{3,2},{4,5},{5,4},{6,7},{7,6},{8,9},{9,8},{10,11... | collective-permute-start | bytes 331784 | tf_op jit(solution)/shard_map/ppermute | solution.py:16
  455.9 6.7 %collective-permute-start.14 = (bf16[24,2304]{1,0:T(8,128)(2,1)S(1)}, bf16[24,2304]{1,0:T(8,128)(2,1)S(1)}, u32[]{:S(2)}, u32[]{:S(2)}) collective-permute-start(bf16[24,2304]{1,0:T(8,128)(2,1)S(1)} %get-tuple-element.60), channel_id=1, source_target_pairs={{0,3},{1,2},{2,1},{3,0},{4,7},{5,6},{6,5},{7,4},{8,11},{9,10},{10,... | collective-permute-start | bytes 331784 | tf_op jit(solution)/shard_map/ppermute | solution.py:16
  455.9 9.6 %collective-permute-start.13 = (bf16[24,2304]{1,0:T(8,128)(2,1)S(1)}, bf16[24,2304]{1,0:T(8,128)(2,1)S(1)}, u32[]{:S(2)}, u32[]{:S(2)}) collective-permute-start(bf16[24,2304]{1,0:T(8,128)(2,1)S(1)} %get-tuple-element.61), channel_id=1, source_target_pairs={{0,2},{1,3},{2,0},{3,1},{4,6},{5,7},{6,4},{7,5},{8,10},{9,11},{10,... | collective-permute-start | bytes 331784 | tf_op jit(solution)/shard_map/ppermute | solution.py:16
  465.6 6.2 %collective-permute-start.15 = (bf16[24,2304]{1,0:T(8,128)(2,1)S(1)}, bf16[24,2304]{1,0:T(8,128)(2,1)S(1)}, u32[]{:S(2)}, u32[]{:S(2)}) collective-permute-start(bf16[24,2304]{1,0:T(8,128)(2,1)S(1)} %get-tuple-element.30), channel_id=1, source_target_pairs={{0,1},{1,0},{2,3},{3,2},{4,5},{5,4},{6,7},{7,6},{8,9},{9,8},{10,11... | collective-permute-start | bytes 331784 | tf_op jit(solution)/shard_map/ppermute | solution.py:16
  465.8 30.2 %collective-permute-start.40 = (bf16[1,768,768]{2,1,0:T(8,128)(2,1)S(1)}, bf16[1,768,768]{2,1,0:T(8,128)(2,1)S(1)}, u32[]{:S(2)}, u32[]{:S(2)}) collective-permute-start(bf16[1,768,768]{2,1,0:T(8,128)(2,1)S(1)} %dynamic-slice_convert_fusion.3), channel_id=1, source_target_pairs={{0,8},{4,12},{8,0},{12,4},{1,9},{5,13},{9,1},{13,5},{2,10},{6,14},... | collective-permute-start | bytes 3538952 | tf_op jit(solution)/shard_map/ppermute | solution.py:16
  467.4 10.1 %collective-permute-start.16 = (bf16[24,2304]{1,0:T(8,128)(2,1)S(1)}, bf16[24,2304]{1,0:T(8,128)(2,1)S(1)}, u32[]{:S(2)}, u32[]{:S(2)}) collective-permute-start(bf16[24,2304]{1,0:T(8,128)(2,1)S(1)} %get-tuple-element.30), channel_id=1, source_target_pairs={{0,2},{1,3},{2,0},{3,1},{4,6},{5,7},{6,4},{7,5},{8,10},{9,11},{10,... | collective-permute-start | bytes 331784 | tf_op jit(solution)/shard_map/ppermute | solution.py:16
  470.1 7.4 %collective-permute-start.17 = (bf16[24,2304]{1,0:T(8,128)(2,1)S(1)}, bf16[24,2304]{1,0:T(8,128)(2,1)S(1)}, u32[]{:S(2)}, u32[]{:S(2)}) collective-permute-start(bf16[24,2304]{1,0:T(8,128)(2,1)S(1)} %get-tuple-element.30), channel_id=1, source_target_pairs={{0,3},{1,2},{2,1},{3,0},{4,7},{5,6},{6,5},{7,4},{8,11},{9,10},{10,... | collective-permute-start | bytes 331784 | tf_op jit(solution)/shard_map/ppermute | solution.py:16
  477.5 20.3 %collective-permute-start.18 = (bf16[96,2304]{1,0:T(8,128)(2,1)S(1)}, bf16[96,2304]{1,0:T(8,128)(2,1)S(1)}, u32[]{:S(2)}, u32[]{:S(2)}) collective-permute-start(bf16[96,2304]{1,0:T(8,128)(2,1)S(1)} %constant_dynamic-update-slice_fusion.18), channel_id=1, source_target_pairs={{0,16},{16,0},{1,17},{17,1},{2,18},{18,2},{3,19},{19,3},{4,20},{20... | collective-permute-start | bytes 1327112 | tf_op jit(solution)/shard_map/ppermute | solution.py:16
  478.8 23.6 %collective-permute-start.31 = (bf16[96,3072]{1,0:T(8,128)(2,1)S(1)}, bf16[96,3072]{1,0:T(8,128)(2,1)S(1)}, u32[]{:S(2)}, u32[]{:S(2)}) collective-permute-start(bf16[96,3072]{1,0:T(8,128)(2,1)S(1)} %fusion.71), channel_id=1, source_target_pairs={{0,16},{16,0},{1,17},{17,1},{2,18},{18,2},{3,19},{19,3},{4,20},{20... | collective-permute-start | bytes 1769480 | tf_op jit(solution)/shard_map/ppermute | solution.py:16
  496.3 15.5 %collective-permute-start.41 = (bf16[384,768]{1,0:T(8,128)(2,1)S(1)}, bf16[384,768]{1,0:T(8,128)(2,1)S(1)}, u32[]{:S(2)}, u32[]{:S(2)}) collective-permute-start(bf16[384,768]{1,0:T(8,128)(2,1)S(1)} %fusion.72), channel_id=1, source_target_pairs={{0,16},{16,0},{1,17},{17,1},{2,18},{18,2},{3,19},{19,3},{4,20},{20... | collective-permute-start | bytes 1769480 | tf_op jit(solution)/shard_map/ppermute | solution.py:16
  502.5 15.9 %collective-permute-start.32 = (bf16[24,3072]{1,0:T(8,128)(2,1)S(1)}, bf16[24,3072]{1,0:T(8,128)(2,1)S(1)}, u32[]{:S(2)}, u32[]{:S(2)}) collective-permute-start(bf16[24,3072]{1,0:T(8,128)(2,1)S(1)} %get-tuple-element.56), channel_id=1, source_target_pairs={{0,1},{1,0},{2,3},{3,2},{4,5},{5,4},{6,7},{7,6},{8,9},{9,8},{10,11... | collective-permute-start | bytes 442376 | tf_op jit(solution)/shard_map/ppermute | solution.py:16
  505.3 13.1 %collective-permute-start.34 = (bf16[24,3072]{1,0:T(8,128)(2,1)S(1)}, bf16[24,3072]{1,0:T(8,128)(2,1)S(1)}, u32[]{:S(2)}, u32[]{:S(2)}) collective-permute-start(bf16[24,3072]{1,0:T(8,128)(2,1)S(1)} %get-tuple-element.57), channel_id=1, source_target_pairs={{0,3},{1,2},{2,1},{3,0},{4,7},{5,6},{6,5},{7,4},{8,11},{9,10},{10,... | collective-permute-start | bytes 442376 | tf_op jit(solution)/shard_map/ppermute | solution.py:16
  508.0 10.5 %collective-permute-start.33 = (bf16[24,3072]{1,0:T(8,128)(2,1)S(1)}, bf16[24,3072]{1,0:T(8,128)(2,1)S(1)}, u32[]{:S(2)}, u32[]{:S(2)}) collective-permute-start(bf16[24,3072]{1,0:T(8,128)(2,1)S(1)} %get-tuple-element.58), channel_id=1, source_target_pairs={{0,2},{1,3},{2,0},{3,1},{4,6},{5,7},{6,4},{7,5},{8,10},{9,11},{10,... | collective-permute-start | bytes 442376 | tf_op jit(solution)/shard_map/ppermute | solution.py:16
  512.0 9.5 %collective-permute-start.42 = (bf16[96,768]{1,0:T(8,128)(2,1)S(1)}, bf16[96,768]{1,0:T(8,128)(2,1)S(1)}, u32[]{:S(2)}, u32[]{:S(2)}) collective-permute-start(bf16[96,768]{1,0:T(8,128)(2,1)S(1)} %get-tuple-element.53), channel_id=1, source_target_pairs={{0,1},{1,0},{2,3},{3,2},{4,5},{5,4},{6,7},{7,6},{8,9},{9,8},{10,11... | collective-permute-start | bytes 442376 | tf_op jit(solution)/shard_map/ppermute | solution.py:16
  515.5 12.2 %collective-permute-start.44 = (bf16[96,768]{1,0:T(8,128)(2,1)S(1)}, bf16[96,768]{1,0:T(8,128)(2,1)S(1)}, u32[]{:S(2)}, u32[]{:S(2)}) collective-permute-start(bf16[96,768]{1,0:T(8,128)(2,1)S(1)} %get-tuple-element.54), channel_id=1, source_target_pairs={{0,3},{1,2},{2,1},{3,0},{4,7},{5,6},{6,5},{7,4},{8,11},{9,10},{10,... | collective-permute-start | bytes 442376 | tf_op jit(solution)/shard_map/ppermute | solution.py:16
  518.5 20.6 %collective-permute-start.43 = (bf16[96,768]{1,0:T(8,128)(2,1)S(1)}, bf16[96,768]{1,0:T(8,128)(2,1)S(1)}, u32[]{:S(2)}, u32[]{:S(2)}) collective-permute-start(bf16[96,768]{1,0:T(8,128)(2,1)S(1)} %get-tuple-element.55), channel_id=1, source_target_pairs={{0,2},{1,3},{2,0},{3,1},{4,6},{5,7},{6,4},{7,5},{8,10},{9,11},{10,... | collective-permute-start | bytes 442376 | tf_op jit(solution)/shard_map/ppermute | solution.py:16
  518.6 26.7 %collective-permute-start.36 = (bf16[24,3072]{1,0:T(8,128)(2,1)S(1)}, bf16[24,3072]{1,0:T(8,128)(2,1)S(1)}, u32[]{:S(2)}, u32[]{:S(2)}) collective-permute-start(bf16[24,3072]{1,0:T(8,128)(2,1)S(1)} %get-tuple-element.26), channel_id=1, source_target_pairs={{0,2},{1,3},{2,0},{3,1},{4,6},{5,7},{6,4},{7,5},{8,10},{9,11},{10,... | collective-permute-start | bytes 442376 | tf_op jit(solution)/shard_map/ppermute | solution.py:16
  521.6 20.6 %collective-permute-start.35 = (bf16[24,3072]{1,0:T(8,128)(2,1)S(1)}, bf16[24,3072]{1,0:T(8,128)(2,1)S(1)}, u32[]{:S(2)}, u32[]{:S(2)}) collective-permute-start(bf16[24,3072]{1,0:T(8,128)(2,1)S(1)} %get-tuple-element.26), channel_id=1, source_target_pairs={{0,1},{1,0},{2,3},{3,2},{4,5},{5,4},{6,7},{7,6},{8,9},{9,8},{10,11... | collective-permute-start | bytes 442376 | tf_op jit(solution)/shard_map/ppermute | solution.py:16
  521.6 23.7 %collective-permute-start.37 = (bf16[24,3072]{1,0:T(8,128)(2,1)S(1)}, bf16[24,3072]{1,0:T(8,128)(2,1)S(1)}, u32[]{:S(2)}, u32[]{:S(2)}) collective-permute-start(bf16[24,3072]{1,0:T(8,128)(2,1)S(1)} %get-tuple-element.26), channel_id=1, source_target_pairs={{0,3},{1,2},{2,1},{3,0},{4,7},{5,6},{6,5},{7,4},{8,11},{9,10},{10,... | collective-permute-start | bytes 442376 | tf_op jit(solution)/shard_map/ppermute | solution.py:16
  539.2 14.0 %collective-permute-start.46 = (bf16[96,768]{1,0:T(8,128)(2,1)S(1)}, bf16[96,768]{1,0:T(8,128)(2,1)S(1)}, u32[]{:S(2)}, u32[]{:S(2)}) collective-permute-start(bf16[96,768]{1,0:T(8,128)(2,1)S(1)} %get-tuple-element.24), channel_id=1, source_target_pairs={{0,2},{1,3},{2,0},{3,1},{4,6},{5,7},{6,4},{7,5},{8,10},{9,11},{10,... | collective-permute-start | bytes 442376 | tf_op jit(solution)/shard_map/ppermute | solution.py:16
  539.2 6.8 %collective-permute-start.45 = (bf16[96,768]{1,0:T(8,128)(2,1)S(1)}, bf16[96,768]{1,0:T(8,128)(2,1)S(1)}, u32[]{:S(2)}, u32[]{:S(2)}) collective-permute-start(bf16[96,768]{1,0:T(8,128)(2,1)S(1)} %get-tuple-element.24), channel_id=1, source_target_pairs={{0,1},{1,0},{2,3},{3,2},{4,5},{5,4},{6,7},{7,6},{8,9},{9,8},{10,11... | collective-permute-start | bytes 442376 | tf_op jit(solution)/shard_map/ppermute | solution.py:16
  542.2 11.0 %collective-permute-start.47 = (bf16[96,768]{1,0:T(8,128)(2,1)S(1)}, bf16[96,768]{1,0:T(8,128)(2,1)S(1)}, u32[]{:S(2)}, u32[]{:S(2)}) collective-permute-start(bf16[96,768]{1,0:T(8,128)(2,1)S(1)} %get-tuple-element.24), channel_id=1, source_target_pairs={{0,3},{1,2},{2,1},{3,0},{4,7},{5,6},{6,5},{7,4},{8,11},{9,10},{10,... | collective-permute-start | bytes 442376 | tf_op jit(solution)/shard_map/ppermute | solution.py:16
  545.4 12.2 %collective-permute-start.38 = (bf16[96,3072]{1,0:T(8,128)(2,1)S(1)}, bf16[96,3072]{1,0:T(8,128)(2,1)S(1)}, u32[]{:S(2)}, u32[]{:S(2)}) collective-permute-start(bf16[96,3072]{1,0:T(8,128)(2,1)S(1)} %constant_dynamic-update-slice_fusion.6), channel_id=1, source_target_pairs={{0,16},{16,0},{1,17},{17,1},{2,18},{18,2},{3,19},{19,3},{4,20},{20... | collective-permute-start | bytes 1769480 | tf_op jit(solution)/shard_map/ppermute | solution.py:16
  553.3 14.7 %collective-permute-start.48 = (bf16[384,768]{1,0:T(8,128)(2,1)S(1)}, bf16[384,768]{1,0:T(8,128)(2,1)S(1)}, u32[]{:S(2)}, u32[]{:S(2)}) collective-permute-start(bf16[384,768]{1,0:T(8,128)(2,1)S(1)} %constant_dynamic-update-slice_fusion), channel_id=1, source_target_pairs={{0,16},{16,0},{1,17},{17,1},{2,18},{18,2},{3,19},{19,3},{4,20},{20... | collective-permute-start | bytes 1769480 | tf_op jit(solution)/shard_map/ppermute | solution.py:16
  (107 other events, 1011.0 us)
Sparse Core Ops, SparseCore 0:
  9.6 33.4 all-gather.6
  44.7 17.4 all-gather.8
  63.7 37.4 all-gather.10
  102.6 37.4 all-gather.12
